TPU v7x, 128 devices: a whole 4x4x4 slice. The times are simulated.
128 devices in a mesh: space: 16 (over z_lo, y, core), dir: 4 (over x), band: 2 (over z_hi).
Axes of the slice: x: 4, y: 4, z: 4 (z_hi: 2, z_lo: 2; z = z_hi * 2 + z_lo), core: 2. Of those that a mesh axis runs over, the one named last changes fastest.
Arguments:
- adjoint_start: float32 [64, 32, 96, 1152], P('dir', 'band', 'space'), may hold values from 0.5 to 1.5
- primal_deviations: float32 [64, 32, 96, 1152], P('dir', 'band', 'space'), may hold values from 0.5 to 1.5
- density: float32 [96, 1152], P('space'), may hold values from 0 to 1
- material: int32 [96, 1152], P('space'), may hold values from 0 to 3
- rate_table: float32 [4, 32], P(None, 'band'), may hold values from 0.05 to 2
- group_speed: float32 [32], P('band'), may hold values from 0.3 to 3
- heat_capacity: float32 [32], replicated, may hold values from 0.1 to 4, as said below
- objective_weight: float32 [96, 1152], P('space'), may hold values from -6 to 6
Outputs:
- dual_intensity: float32 [64, 32, 96, 1152], P('dir', 'band', 'space')
- design_gradient: float32 [96, 1152], P('space')
Inputs may be any that keep to these rules, and one draw needn't show every extreme that they name: `heat_capacity`: heat capacities of the bands, positive.
All inputs are finite; a program needn't handle non-finite values.
Results may differ from a plain program's by a relative error of at most 0.0003.
Values sent between devices are 32-bit elements; how exact they have to be, the bound alone decides.
A program may use at most 128 MiB of HBM per device.

v0:
```python
import jax
import jax.numpy as jnp
from jax import lax
from jax.sharding import PartitionSpec as P

NDIR = 64
NB = 32
NY = 192
ITERS = 2


def extended(block, sides, width):
    for axis, dim in sides:
        count = lax.axis_size(axis)
        forward = [(i, i + 1) for i in range(count - 1)]
        backward = [(target, source) for source, target in forward]
        low = lax.ppermute(
            lax.slice_in_dim(block, block.shape[dim] - width, None, axis=dim), axis, forward
        )
        high = lax.ppermute(lax.slice_in_dim(block, 0, width, axis=dim), axis, backward)
        block = jnp.concatenate([low, block, high], axis=dim)
    return block


def local_directions(count):
    block = lax.axis_index("dir")
    slot = jnp.arange(count, dtype=jnp.int32)
    half = count // 2
    side = slot // half
    pair = slot % half
    azimuth = jnp.pi * ((block * half + pair).astype(jnp.float32) + 0.5) / (NDIR // 2) - jnp.pi / 2
    along_z = 0.4 * (1.0 - 2.0 * (pair % 2).astype(jnp.float32))
    tilt = jnp.sqrt(1.0 - along_z * along_z)
    along_x = (1.0 - 2.0 * side.astype(jnp.float32)) * tilt * jnp.cos(azimuth)
    along_y = tilt * jnp.sin(azimuth)
    return (along_x, along_y, along_z)


def plane_move(field, offset):
    last = field.ndim - 1
    size = field.shape[last]
    if offset > 0:
        rest = lax.slice_in_dim(field, offset, size, axis=last)
        pad_block = jnp.zeros_like(lax.slice_in_dim(field, 0, offset, axis=last))
        return jnp.concatenate([rest, pad_block], last)
    rest = lax.slice_in_dim(field, 0, size + offset, axis=last)
    pad_block = jnp.zeros_like(lax.slice_in_dim(field, 0, -offset, axis=last))
    return jnp.concatenate([pad_block, rest], last)


def first_neighbours(dual_intensity):
    half = dual_intensity.shape[0] // 2
    padded = extended(dual_intensity, (("space", 2),), 1)
    forward_side = padded[:half, :, 2:]
    backward_side = padded[half:, :, :-2]
    return jnp.concatenate([forward_side, backward_side], axis=0)


def reduce_volumes(partials):
    summed = lax.psum(partials, "band")
    summed = lax.psum(summed, "dir")
    return summed


def on_device(
    adjoint_start,
    primal_deviations,
    density,
    material,
    rate_table,
    group_speed,
    heat_capacity,
    objective_weight,
):
    count = adjoint_start.shape[0]
    bands = adjoint_start.shape[1]
    plane = adjoint_start.shape[3]
    along_x, along_y, along_z = local_directions(count)
    position = jnp.arange(plane, dtype=jnp.int32) % NY
    keep_ahead = (position < NY - 1).astype(jnp.float32)
    keep_behind = (position > 0).astype(jnp.float32)
    speed = group_speed[None, :, None, None]
    speed_x = speed * jnp.abs(along_x)[:, None, None, None]
    speed_y = speed * jnp.abs(along_y)[:, None, None, None]
    speed_z = speed * jnp.abs(along_z)[:, None, None, None]
    rising_y = (along_y > 0)[:, None, None, None]
    rising_z = (along_z > 0)[:, None, None, None]
    indicator = (
        material[None] == jnp.arange(rate_table.shape[0], dtype=jnp.int32)[:, None, None]
    ).astype(jnp.float32)
    base = jnp.einsum("mb,mxp->bxp", rate_table, indicator, precision=lax.Precision.HIGHEST)
    relaxation_frequency = base * (0.2 + 0.8 * density)[None]
    relaxation_slope = 0.8 * base
    local_heat = lax.dynamic_slice_in_dim(heat_capacity, lax.axis_index("band") * bands, bands)
    weights = local_heat / (NDIR * jnp.sum(heat_capacity))
    column = weights[None, :, None, None]
    thermal_share = jnp.sum(column * primal_deviations, axis=(0, 1))
    relaxation_share = jnp.sum(relaxation_frequency[None] * adjoint_start, axis=(0, 1))
    crystal_kelvin, exchange_link = reduce_volumes((thermal_share, relaxation_share))
    diagonal = speed_x + speed_y + speed_z + relaxation_frequency[None]
    cell_source = NDIR * NB * objective_weight
    dual_intensity = adjoint_start
    gradient_part = jnp.zeros_like(density)
    for step in range(ITERS):
        source = column * (exchange_link + cell_source)[None, None]
        near = speed_x * first_neighbours(dual_intensity)
        near = near + speed_y * jnp.where(
            rising_y,
            plane_move(dual_intensity, 1) * keep_ahead,
            plane_move(dual_intensity, -1) * keep_behind,
        )
        near = near + speed_z * jnp.where(
            rising_z, plane_move(dual_intensity, NY), plane_move(dual_intensity, -NY)
        )
        dual_intensity = (source + near) / diagonal
        gradient_part = gradient_part + jnp.sum(
            relaxation_slope[None]
            * dual_intensity
            * (primal_deviations - crystal_kelvin[None, None]),
            axis=(0, 1),
        )
        if step + 1 < ITERS:
            (exchange_link,) = reduce_volumes(
                (jnp.sum(relaxation_frequency[None] * dual_intensity, axis=(0, 1)),)
            )
    (gradient,) = reduce_volumes((gradient_part,))
    return (dual_intensity, gradient * (-0.125 / ITERS))


def solution(mesh):
    placed = (
        P("dir", "band", "space", None),
        P("dir", "band", "space", None),
        P("space", None),
        P("space", None),
        P(None, "band"),
        P("band"),
        P(),
        P("space", None),
    )
    return jax.shard_map(
        on_device,
        mesh=mesh,
        in_specs=placed,
        out_specs=(P("dir", "band", "space", None), P("space", None)),
        check_vma=False,
    )
```

profile of v0, /device:TPU:32, one launch (start us, length us, event | category | flops | bytes accessed | tf_op | source)
XLA Modules:
  0.0 198.8 jit_solution(13606935609989549067)
XLA Ops:
  0.6 0.0 copy-start
  0.6 3.2 %fusion.36 = (f32[16,16,1,1152]{3,1,2,0:T(8,128)}, f32[16,16,1,1152]{3,1,2,0:T(8,128)}) fusion(f32[16,16,6,1152]{3,1,2,0:T(8,128)} %param.8), kind=kLoop, calls=%fused_computation.78 | loop fusion | bytes 4718592 | tf_op jit(solution)/shard_map/slice | solution.py:20
  3.9 3.9 %collective-permute-start = (f32[16,16,1,1152]{3,1,2,0:T(8,128)}, f32[16,16,1,1152]{3,1,2,0:T(8,128)S(1)}, u32[]{:S(2)}, u32[]{:S(2)}) collective-permute-start(f32[16,16,1,1152]{3,1,2,0:T(8,128)} %get-tuple-element.17), channel_id=1, source_target_pairs={{8,0},{16,8},{24,16},{32,24},{40,32},{48,40},{56,48},{64,56},{72,6... | collective-permute-start | bytes 3538952 | tf_op jit(solution)/shard_map/ppermute | solution.py:20
  7.8 1.9 collective-permute-start.1
  9.7 0.1 broadcast_compare_fusion
  9.9 0.0 copy-start.4
  9.9 0.0 copy-start.5
  9.9 11.2 %fusion.38 = (f32[16,16,6,960]{3,1,2,0:T(8,128)}, f32[16,16,6,960]{3,1,2,0:T(8,128)}) fusion(f32[16,16,6,1152]{3,1,2,0:T(8,128)} %param.8), kind=kLoop, calls=%fused_computation.80 | loop fusion | bytes 23592960 | tf_op jit(solution)/shard_map/slice | solution.py:43
  21.1 0.0 copy-start.7
  21.1 0.0 copy-done.4
  21.1 0.0 copy-done
  21.1 0.0 copy-done.5
  21.1 0.4 multiply_bitcast_fusion
  21.5 0.0 copy-start.3
  21.5 0.0 copy-start.6
  21.6 3.6 %multiply_reduce_fusion.4 = f32[6,1152]{1,0:T(8,128)S(1)} fusion(f32[16,16,6,1152]{3,1,2,0:T(8,128)} %param.8, f32[16,6,1152]{2,0,1:T(8,128)S(1)} %get-tuple-element.24), kind=kLoop, calls=%fused_computation.22 | loop fusion | flops 3532032 | bytes 7547904 | tf_op jit(solution)/shard_map/reduce_sum | solution.py:98
  25.2 11.8 %psum.56 = f32[6,1152]{1,0:T(8,128)S(1)} all-reduce(f32[6,1152]{1,0:T(8,128)S(1)} %multiply_reduce_fusion.4), channel_id=1, replica_groups=mesh['space'=16,'dir'=4,'band'=2] {'band'}, use_global_device_ids=true, to_apply=%region_2.3 | all-reduce | flops 6912 | bytes 55296 | tf_op jit(solution)/shard_map/psum | solution.py:60
  37.0 17.3 %psum.57 = f32[6,1152]{1,0:T(8,128)S(1)} all-reduce(f32[6,1152]{1,0:T(8,128)S(1)} %psum.56), channel_id=1, replica_groups=mesh['space'=16,'dir'=4,'band'=2] {'dir'}, use_global_device_ids=true, to_apply=%region_3.4 | all-reduce | flops 6912 | bytes 55296 | tf_op jit(solution)/shard_map/psum | solution.py:61
  54.4 0.0 copy-done.7
  54.4 0.6 reduce_sum.54
  55.6 0.1 dynamic-slice_divide_fusion
  55.7 3.6 %multiply_reduce_fusion.2 = f32[6,1152]{1,0:T(8,128)S(1)} fusion(f32[16,16,6,1152]{3,1,2,0:T(8,128)} %param.9, f32[16]{0:T(128)S(1)} %dynamic-slice_divide_fusion), kind=kLoop, calls=%fused_computation.20 | loop fusion | flops 3532032 | bytes 7105600 | tf_op jit(solution)/shard_map/reduce_sum | solution.py:97
  59.3 0.0 copy-done.3
  59.3 0.1 broadcast_multiply_fusion.1
  59.5 0.0 copy-done.6
  59.5 0.1 broadcast_multiply_fusion.5
  59.5 12.4 %fusion.37 = (f32[16,16,6,1151]{3,1,2,0:T(8,128)}, f32[16,16,6,1151]{3,1,2,0:T(8,128)}) fusion(f32[16,16,6,1152]{3,1,2,0:T(8,128)} %param.8), kind=kLoop, calls=%fused_computation.79 | loop fusion | bytes 28286976 | tf_op jit(solution)/shard_map/slice | solution.py:43
  71.9 0.0 collective-permute-done
  71.9 0.0 collective-permute-done.1
  71.9 14.3 %multiply_reduce_fusion.3 = (f32[6,1152]{1,0:T(8,128)S(1)}, f32[16,16,6,1152]{3,1,2,0:T(8,128)S(1)}) fusion(f32[16,6,1152]{2,0,1:T(8,128)S(1)} %get-tuple-element.24, f32[16,16]{1,0:T(8,128)S(1)} %get-tuple-element.26, f32[16,16,6,960]{3,1,2,0:T(8,128)} %get-tuple-element.22, f32[16,16,6,960]{3,1,2,0:T(8,128)} %get-tuple-element.21, ...), kind=kLoop, calls=%fused_computation.21 | loop fusion | flops 40690944 | bytes 43380768 | tf_op jit(solution)/shard_map/reduce_sum | solution.py:124
  86.2 0.0 copy-start.2
  86.2 2.9 %copy-done.2 = f32[16,16,6,1152]{3,1,2,0:T(8,128)} copy-done((f32[16,16,6,1152]{3,1,2,0:T(8,128)}, f32[16,16,6,1152]{3,1,2,0:T(8,128)S(1)}, u32[]{:S(2)}) %copy-start.2) | copy-done | bytes 7077912
  89.1 1.6 fusion.33
  90.7 10.9 %fusion.35 = (f32[16,16,6,960]{3,1,2,0:T(8,128)}, f32[16,16,6,960]{3,1,2,0:T(8,128)}) fusion(f32[16,16,6,1152]{3,1,2,0:T(8,128)} %copy-done.2), kind=kLoop, calls=%fused_computation.77 | loop fusion | bytes 23592960 | tf_op jit(solution)/shard_map/slice | solution.py:43
  101.6 9.0 %all-reduce.9 = (f32[6,1152]{1,0:T(8,128)S(1)}, f32[6,1152]{1,0:T(8,128)S(1)}) all-reduce(f32[6,1152]{1,0:T(8,128)S(1)} %get-tuple-element.9, f32[6,1152]{1,0:T(8,128)S(1)} %multiply_reduce_fusion.2), channel_id=1, replica_groups=mesh['space'=16,'dir'=4,'band'=2] {'band'}, use_global_device_ids=true, to_apply=%region_5.6 | all-reduce | flops 13824 | bytes 110592 | tf_op jit(solution)/shard_map/psum | solution.py:60
  110.6 15.3 %all-reduce.8 = (f32[6,1152]{1,0:T(8,128)S(1)}, f32[6,1152]{1,0:T(8,128)S(1)}) all-reduce(f32[6,1152]{1,0:T(8,128)S(1)} %get-tuple-element.6, f32[6,1152]{1,0:T(8,128)S(1)} %get-tuple-element.7), channel_id=1, replica_groups=mesh['space'=16,'dir'=4,'band'=2] {'dir'}, use_global_device_ids=true, to_apply=%region_6.7 | all-reduce | flops 13824 | bytes 110592 | tf_op jit(solution)/shard_map/psum | solution.py:61
  125.9 0.1 broadcast_multiply_fusion
  126.0 1.9 collective-permute-start.2
  128.0 2.4 %collective-permute-start.3 = (f32[16,16,1,1152]{3,1,2,0:T(8,128)}, f32[16,16,1,1152]{3,1,2,0:T(8,128)}, u32[]{:S(2)}, u32[]{:S(2)}) collective-permute-start(f32[16,16,1,1152]{3,1,2,0:T(8,128)} %get-tuple-element.12), channel_id=1, source_target_pairs={{0,8},{8,16},{16,24},{24,32},{32,40},{40,48},{48,56},{56,64},{64,7... | collective-permute-start | bytes 3538952 | tf_op jit(solution)/shard_map/ppermute | solution.py:17
  130.4 11.9 %fusion.34 = (f32[16,16,6,1151]{3,1,2,0:T(8,128)}, f32[16,16,6,1151]{3,1,2,0:T(8,128)}) fusion(f32[16,16,6,1152]{3,1,2,0:T(8,128)} %copy-done.2), kind=kLoop, calls=%fused_computation.76 | loop fusion | bytes 28286976 | tf_op jit(solution)/shard_map/slice | solution.py:43
  142.3 0.0 collective-permute-done.2
  142.3 5.6 %collective-permute-done.3 = f32[16,16,1,1152]{3,1,2,0:T(8,128)} collective-permute-done((f32[16,16,1,1152]{3,1,2,0:T(8,128)}, f32[16,16,1,1152]{3,1,2,0:T(8,128)}, u32[]{:S(2)}, u32[]{:S(2)}) %collective-permute-start.3) | collective-permute-done | bytes 1179680 | tf_op jit(solution)/shard_map/ppermute | solution.py:17
  147.9 0.0 copy-start.1
  147.9 21.8 %multiply_reduce_fusion = (f32[6,1152]{1,0:T(8,128)S(1)}, f32[6,1152]{1,0:T(8,128)S(1)}, f32[16,16,6,1152]{3,1,2,0:T(8,128)}) fusion(f32[16,16,6,1152]{3,1,2,0:T(8,128)} %param.9, f32[6,1152]{1,0:T(8,128)S(1)} %get-tuple-element.5, f32[16,6,1152]{2,0,1:T(8,128)S(1)} %get-tuple-element.23, f32[16,16,6,1152]{3,1,2,0:T(8,128)} %copy-done.2, ...), kind=kLoop, calls=%fused_computation.18 | loop fusion | flops 49531392 | bytes 50956320 | tf_op jit(solution)/shard_map/reduce_sum | solution.py:116
  169.8 11.8 %psum.62 = f32[6,1152]{1,0:T(8,128)S(1)} all-reduce(f32[6,1152]{1,0:T(8,128)S(1)} %add.252), channel_id=1, replica_groups=mesh['space'=16,'dir'=4,'band'=2] {'band'}, use_global_device_ids=true, to_apply=%region_12.13 | all-reduce | flops 6912 | bytes 55296 | tf_op jit(solution)/shard_map/psum | solution.py:60
  181.6 16.5 %psum.63 = f32[6,1152]{1,0:T(8,128)S(1)} all-reduce(f32[6,1152]{1,0:T(8,128)S(1)} %psum.62), channel_id=1, replica_groups=mesh['space'=16,'dir'=4,'band'=2] {'dir'}, use_global_device_ids=true, to_apply=%region_13.14 | all-reduce | flops 6912 | bytes 55296 | tf_op jit(solution)/shard_map/psum | solution.py:61
  198.2 0.6 broadcast_multiply_fusion.2
  198.8 0.0 copy-done.1
  (7 shorter events, 0.1 us)
Async XLA Ops:
  0.6 20.5 %copy-start = (f32[4,16]{1,0:T(4,128)S(1)}, f32[4,16]{1,0:T(4,128)}, u32[]{:S(2)}) copy-start(f32[4,16]{1,0:T(4,128)} %param.12) | copy-start | bytes 772
  3.9 68.0 %collective-permute-start = (f32[16,16,1,1152]{3,1,2,0:T(8,128)}, f32[16,16,1,1152]{3,1,2,0:T(8,128)S(1)}, u32[]{:S(2)}, u32[]{:S(2)}) collective-permute-start(f32[16,16,1,1152]{3,1,2,0:T(8,128)} %get-tuple-element.17), channel_id=1, source_target_pairs={{8,0},{16,8},{24,16},{32,24},{40,32},{48,40},{56,48},{64,56},{72,6... | collective-permute-start | bytes 3538952 | tf_op jit(solution)/shard_map/ppermute | solution.py:20
  7.8 64.1 %collective-permute-start.1 = (f32[16,16,1,1152]{3,1,2,0:T(8,128)}, f32[16,16,1,1152]{3,1,2,0:T(8,128)}, u32[]{:S(2)}, u32[]{:S(2)}) collective-permute-start(f32[16,16,1,1152]{3,1,2,0:T(8,128)} %get-tuple-element.18), channel_id=1, source_target_pairs={{0,8},{8,16},{16,24},{24,32},{32,40},{40,48},{48,56},{56,64},{64,7... | collective-permute-start | bytes 3538952 | tf_op jit(solution)/shard_map/ppermute | solution.py:17
  9.9 11.2 %copy-start.4 = (f32[6,1152]{1,0:T(8,128)S(1)}, f32[6,1152]{1,0:T(8,128)}, u32[]{:S(2)}) copy-start(f32[6,1152]{1,0:T(8,128)} %param.10) | copy-start | bytes 82948
  9.9 11.2 %copy-start.5 = (s32[6,1152]{1,0:T(8,128)S(1)}, s32[6,1152]{1,0:T(8,128)}, u32[]{:S(2)}) copy-start(s32[6,1152]{1,0:T(8,128)} %param.11) | copy-start | bytes 82948
  21.1 33.3 %copy-start.7 = (f32[32]{0:T(128)S(1)}, f32[32]{0:T(128)}, u32[]{:S(2)}) copy-start(f32[32]{0:T(128)} %param.14) | copy-start | bytes 388
  21.5 37.8 %copy-start.3 = (f32[6,1152]{1,0:T(8,128)S(1)}, f32[6,1152]{1,0:T(8,128)}, u32[]{:S(2)}) copy-start(f32[6,1152]{1,0:T(8,128)} %param.15) | copy-start | bytes 82948
  21.5 37.9 %copy-start.6 = (f32[16]{0:T(128)S(1)}, f32[16]{0:T(128)}, u32[]{:S(2)}) copy-start(f32[16]{0:T(128)} %param.13) | copy-start | bytes 196
  86.2 2.9 %copy-start.2 = (f32[16,16,6,1152]{3,1,2,0:T(8,128)}, f32[16,16,6,1152]{3,1,2,0:T(8,128)S(1)}, u32[]{:S(2)}) copy-start(f32[16,16,6,1152]{3,1,2,0:T(8,128)S(1)} %get-tuple-element.10) | copy-start | bytes 21233668
  126.0 16.3 %collective-permute-start.2 = (f32[16,16,1,1152]{3,1,2,0:T(8,128)}, f32[16,16,1,1152]{3,1,2,0:T(8,128)S(1)}, u32[]{:S(2)}, u32[]{:S(2)}) collective-permute-start(f32[16,16,1,1152]{3,1,2,0:T(8,128)} %get-tuple-element.11), channel_id=1, source_target_pairs={{8,0},{16,8},{24,16},{32,24},{40,32},{48,40},{56,48},{64,56},{72,6... | collective-permute-start | bytes 3538952 | tf_op jit(solution)/shard_map/ppermute | solution.py:20
  128.0 19.9 %collective-permute-start.3 = (f32[16,16,1,1152]{3,1,2,0:T(8,128)}, f32[16,16,1,1152]{3,1,2,0:T(8,128)}, u32[]{:S(2)}, u32[]{:S(2)}) collective-permute-start(f32[16,16,1,1152]{3,1,2,0:T(8,128)} %get-tuple-element.12), channel_id=1, source_target_pairs={{0,8},{8,16},{16,24},{24,32},{32,40},{40,48},{48,56},{56,64},{64,7... | collective-permute-start | bytes 3538952 | tf_op jit(solution)/shard_map/ppermute | solution.py:17
  147.9 50.9 %copy-start.1 = (f32[4,16]{1,0:T(4,128)S(1)}, f32[4,16]{1,0:T(4,128)}, u32[]{:S(2)}) copy-start(f32[4,16]{1,0:T(4,128)} %param.12) | copy-start | bytes 772
where the time goes:
time: 199 us
  blocking collectives  81.8 us (41%)
  local copies, waits for them, and re-layouts  54.2 us (27%)
  other arithmetic  45.1 us (23%)
  starting transfers between devices  10.1 us (5%)
  waiting for transfers between devices  5.61 us (3%)
    psum x3, blocking collectives, reduce_volumes(): summed = lax.psum(summed, 'dir')  49.1 us
    slice x4, local copies, waits for them, and re-layouts, plane_move(): rest = lax.slice_in_dim(field, offset, size, axis=last)  46.5 us
    psum x3, blocking collectives, reduce_volumes(): summed = lax.psum(partials, 'band')  32.7 us
    reduce_sum x1, other arithmetic, on_device(): jnp.sum(relaxation_slope[None] * dual_intensity * (primal_deviations - cr...  21.8 us
    reduce_sum x1, other arithmetic, on_device(): jnp.sum(relaxation_frequency[None] * dual_intensity, axis=(0, 1))  14.3 us
    ppermute x2, starting transfers between devices, extended(): lax.ppermute(lax.slice_in_dim(block, 0, width, axis=dim), axis, backward)  5.81 us
    ppermute x2, waiting for transfers between devices, extended(): lax.ppermute(lax.slice_in_dim(block, block.shape[dim] - width, None, axis...  5.61 us
    slice x2, local copies, waits for them, and re-layouts, extended(): lax.slice_in_dim(block, 0, width, axis=dim)  4.81 us
  transfers between devices with their start and end apart: 4, of which 1 were waited for; matrix products, arithmetic and copies ran while one was open for 22% of the time, Pallas kernels for 0%

commit v1 on v0

v1 whole, which is shorter than its diff:
```python
import jax
import jax.numpy as jnp
import numpy as np
from jax import lax
from jax.experimental import pallas as pl
from jax.experimental.pallas import tpu as pltpu
from jax.sharding import PartitionSpec as P

NDIR = 64
NB = 32
NY = 192
ITERS = 2
LANES = 128
SUB = 8
MESH = pl.DeviceIdType.MESH


def direction_constants(half, blocks):
    index = np.arange(blocks * half, dtype=np.float32)
    azimuth = np.float32(np.pi) * (index + np.float32(0.5)) / np.float32(NDIR // 2)
    azimuth = azimuth - np.float32(np.pi / 2)
    pair = np.arange(blocks * half) % half
    along_z = np.float32(0.4) * (1 - 2 * (pair % 2)).astype(np.float32)
    tilt = np.sqrt(np.float32(1.0) - along_z * along_z)
    along_x = np.abs(tilt * np.cos(azimuth))
    along_y = np.abs(tilt * np.sin(azimuth))
    return (
        along_x.reshape(blocks, half),
        along_y.reshape(blocks, half),
        np.abs(along_z).reshape(blocks, half),
    )


def by_block(block, values):
    chosen = jnp.float32(values[-1])
    for index in range(len(values) - 2, -1, -1):
        chosen = jnp.where(block == index, jnp.float32(values[index]), chosen)
    return chosen


def make_kernel(ndir, nbands, nx, plane, n_space, n_dir, n_band):
    half = ndir // 2
    tiles = plane // LANES
    subs = nbands // SUB
    last = nx - 1
    const_x, const_y, const_z = direction_constants(half, n_dir)

    def kernel(
        adj, pri, den, mat, rt, gs, hc, ow,
        out, grad,
        A, PV, D, R, RATE, BASE, WS, CF, SUMA, SUMP, TB, ACCB, ACCG,
        denv, matv, rtv, gsv, hcv, owv, gradv,
        XB, ZB,
        load_sem, small_sem, h_send, h_recv, x_send, x_recv, z_send, z_recv, out_sem, grad_sem,
    ):
        space = lax.axis_index("space")
        block = lax.axis_index("dir")
        band = lax.axis_index("band")
        other_band = 1 - band

        barrier = pltpu.get_barrier_semaphore()
        for k in range(1, n_dir):
            peer = lax.rem(block + k, n_dir)
            pl.semaphore_signal(barrier, inc=1, device_id={"dir": peer}, device_id_type=MESH)
        pl.semaphore_signal(barrier, inc=1, device_id={"band": other_band}, device_id_type=MESH)

        @pl.when(space > 0)
        def _():
            pl.semaphore_signal(barrier, inc=1, device_id={"space": space - 1}, device_id_type=MESH)

        @pl.when(space < n_space - 1)
        def _():
            pl.semaphore_signal(barrier, inc=1, device_id={"space": space + 1}, device_id_type=MESH)

        smalls = [
            pltpu.make_async_copy(src, dst, small_sem.at[i])
            for i, (src, dst) in enumerate(
                ((den, denv), (mat, matv), (rt, rtv), (gs, gsv), (hc, hcv), (ow, owv))
            )
        ]
        group = 4
        loads_a = []
        loads_p = []
        for g in range(ndir // group):
            first = g * group
            shift = 0 if first < half else 1
            loads_a.append(
                pltpu.make_async_copy(
                    adj.at[pl.ds(first, group)],
                    A.at[pl.ds(first, group), pl.ds(shift, nx)],
                    load_sem.at[0, g],
                )
            )
            loads_p.append(
                pltpu.make_async_copy(
                    pri.at[pl.ds(first, group)], PV.at[pl.ds(first, group)], load_sem.at[1, g]
                )
            )
        for copy in smalls:
            copy.start()
        for copy in loads_a:
            copy.start()
        for copy in loads_p:
            copy.start()

        at_end = jnp.logical_or(space == 0, space == n_space - 1)

        @pl.when(at_end)
        def _():
            pl.semaphore_wait(barrier, n_dir + 1)

        @pl.when(jnp.logical_not(at_end))
        def _():
            pl.semaphore_wait(barrier, n_dir + 2)

        def halo(step, down, source=None):
            buffer = D if step else A
            if down:
                src = adj.at[pl.ds(0, half), 0] if step == 0 else D.at[pl.ds(0, half), 0]
                return pltpu.make_async_remote_copy(
                    src_ref=src,
                    dst_ref=buffer.at[pl.ds(0, half), nx],
                    send_sem=h_send.at[step, 0],
                    recv_sem=h_recv.at[step, 0],
                    device_id={"space": space - 1},
                    device_id_type=MESH,
                )
            src = adj.at[pl.ds(half, half), last] if step == 0 else D.at[pl.ds(half, half), nx]
            return pltpu.make_async_remote_copy(
                src_ref=src,
                dst_ref=buffer.at[pl.ds(half, half), 0],
                send_sem=h_send.at[step, 1],
                recv_sem=h_recv.at[step, 1],
                device_id={"space": space + 1},
                device_id_type=MESH,
            )

        def halo_start(step):
            @pl.when(space > 0)
            def _():
                halo(step, True).start()

            @pl.when(space < n_space - 1)
            def _():
                halo(step, False).start()

        def halo_wait_recv(step):
            @pl.when(space < n_space - 1)
            def _():
                halo(step, True).wait_recv()

            @pl.when(space > 0)
            def _():
                halo(step, False).wait_recv()

        def halo_wait_send(step):
            @pl.when(space > 0)
            def _():
                halo(step, True).wait_send()

            @pl.when(space < n_space - 1)
            def _():
                halo(step, False).wait_send()

        halo_start(0)

        @pl.when(space == n_space - 1)
        def _():
            def clear(d, carry):
                A[d, nx] = jnp.zeros((nbands, plane), jnp.float32)
                D[d, nx] = jnp.zeros((nbands, plane), jnp.float32)
                return carry

            lax.fori_loop(0, half, clear, 0)

        @pl.when(space == 0)
        def _():
            def clear(d, carry):
                A[half + d, 0] = jnp.zeros((nbands, plane), jnp.float32)
                D[half + d, 0] = jnp.zeros((nbands, plane), jnp.float32)
                return carry

            lax.fori_loop(0, half, clear, 0)

        for copy in smalls:
            copy.wait()
        row_index = lax.broadcasted_iota(jnp.int32, (nbands, nbands), 0)
        lane_index = lax.broadcasted_iota(jnp.int32, (nbands, nbands), 1)

        def column(row):
            spread = jnp.where(row_index == lane_index, row, 0.0)
            return jnp.broadcast_to(jnp.sum(spread, axis=1, keepdims=True), (nbands, LANES))

        rates = [column(rtv[m : m + 1, :]) for m in range(rt.shape[0])]
        speed = column(gsv[...])
        heat = hcv[...]
        total_heat = jnp.sum(heat, axis=1, keepdims=True)
        wide_row = lax.broadcasted_iota(jnp.int32, (nbands, NB), 0) + band * nbands
        wide_lane = lax.broadcasted_iota(jnp.int32, (nbands, NB), 1)
        local_heat = jnp.sum(jnp.where(wide_row == wide_lane, heat, 0.0), axis=1, keepdims=True)
        weight = jnp.broadcast_to(local_heat / (NDIR * total_heat), (nbands, LANES))
        lane = lax.broadcasted_iota(jnp.int32, (nbands, LANES), 1)
        ahead = block >= n_dir // 2
        middle = jnp.where(ahead, 63, 64)
        edge = jnp.where(ahead, LANES - 1, 0)
        for pair in range(half):
            sx = speed * by_block(block, const_x[:, pair])
            sy = speed * by_block(block, const_y[:, pair])
            sz = speed * jnp.float32(const_z[0, pair])
            CF[pair, 0] = sx
            CF[pair, 1] = sy
            CF[pair, 2] = jnp.where(lane == middle, 0.0, sy)
            CF[pair, 3] = jnp.where(lane == edge, 0.0, sy)
            CF[pair, 4] = sz
            CF[pair, 5] = sx + sy + sz

        for x in range(nx):
            for j in range(tiles):
                cut = slice(j * LANES, (j + 1) * LANES)
                kind = jnp.broadcast_to(matv[x : x + 1, cut], (nbands, LANES))
                base = rates[-1]
                for m in range(rt.shape[0] - 2, -1, -1):
                    base = jnp.where(kind == m, rates[m], base)
                BASE[x, :, cut] = base
                RATE[x, :, cut] = base * (0.2 + 0.8 * denv[x : x + 1, cut])

        def sum_group(source, target, g, shift):
            def body(x, carry):
                total = source[g * group, x + shift]
                for d in range(1, group):
                    total = total + source[g * group + d, x + shift]
                if g:
                    total = total + target[x]
                target[x] = total
                return carry

            lax.fori_loop(0, nx, body, 0)

        def x_copy(n, k):
            return pltpu.make_async_remote_copy(
                src_ref=XB.at[n, block],
                dst_ref=XB.at[n, block],
                send_sem=x_send.at[n, k - 1],
                recv_sem=x_recv.at[n, k - 1],
                device_id={"dir": lax.rem(block + k, n_dir)},
                device_id_type=MESH,
            )

        def z_copy(n):
            return pltpu.make_async_remote_copy(
                src_ref=ZB.at[n, band],
                dst_ref=ZB.at[n, band],
                send_sem=z_send.at[n],
                recv_sem=z_recv.at[n],
                device_id={"band": other_band},
                device_id_type=MESH,
            )

        def exchange_start(n):
            for k in range(1, n_dir):
                x_copy(n, k).start()

        def exchange_middle(n):
            for k in range(1, n_dir):
                x_copy(n, k).wait_recv()
            total = XB[n, 0]
            for k in range(1, n_dir):
                total = total + XB[n, k]
            ZB[n, band] = total
            z_copy(n).start()

        def exchange_end(n):
            z_copy(n).wait_recv()
            return ZB[n, 0] + ZB[n, 1]

        def exchange_drain(n):
            for k in range(1, n_dir):
                x_copy(n, k).wait_send()
            z_copy(n).wait_send()

        wide_weight = jnp.concatenate([weight] * tiles, axis=1)

        for g in range(ndir // group):
            loads_a[g].wait()
            sum_group(A, SUMA, g, 0 if g * group < half else 1)
        for x in range(nx):
            XB[0, block, x : x + 1, :] = jnp.sum(RATE[x] * SUMA[x], axis=0, keepdims=True)
        exchange_start(0)
        for g in range(ndir // group):
            loads_p[g].wait()
            sum_group(PV, SUMP, g, 0)
        for x in range(nx):
            XB[1, block, x : x + 1, :] = jnp.sum(wide_weight * SUMP[x], axis=0, keepdims=True)
        exchange_start(1)

        def set_source(coupling):
            source = coupling + NDIR * NB * owv[...]
            for x in range(nx):
                WS[x] = wide_weight * source[x : x + 1]

        for x in range(nx):
            ACCB[x] = jnp.zeros((SUB, plane), jnp.float32)
            ACCG[x] = jnp.zeros((SUB, plane), jnp.float32)

        exchange_middle(0)
        exchange_middle(1)
        set_source(exchange_end(0))
        temperature = exchange_end(1)
        for x in range(nx):
            TB[x] = jnp.broadcast_to(temperature[x : x + 1], (SUB, plane))

        low_lanes = lax.broadcasted_iota(jnp.int32, (SUB, LANES), 1) < LANES // 2
        edge_first = lax.broadcasted_iota(jnp.int32, (SUB, LANES), 1) == 0
        edge_last = lax.broadcasted_iota(jnp.int32, (SUB, LANES), 1) == LANES - 1

        def slab(step, forward_y, side, pair, up_z, x, acc_b, acc_g):
            source, target = (A, D) if step == 0 else (D, A)
            d = pair + side * half
            own = x + side
            beside = x + 1 - side
            for s in range(subs):
                rows = pl.ds(s * SUB, SUB)
                field = source[d, own, rows, :]
                near_x = source[d, beside, rows, :]
                cx = CF[pair, 0, rows, :]
                cy = [CF[pair, 1 + i, rows, :] for i in range(3)]
                cz = CF[pair, 4, rows, :]
                csum = CF[pair, 5, rows, :]
                rate = RATE[x, rows, :]
                base = BASE[x, rows, :]
                ws = WS[x, rows, :]
                excess = PV[d, x, rows, :]
                warm = TB[x]
                if step:
                    recip = R[d, x, rows, :]
                cut = [slice(j * LANES, (j + 1) * LANES) for j in range(tiles)]
                parts = [field[:, c] for c in cut]
                turn = [pltpu.roll(v, LANES - 1 if forward_y else 1, 1) for v in parts]
                halfway = [pltpu.roll(v, LANES // 2, 1) for v in parts]
                results = []
                recips = []
                for j in range(tiles):
                    if forward_y:
                        coef = cy[(0, 1, 2)[j % 3]]
                        moved = turn[j]
                        if j % 3 != 2:
                            moved = jnp.where(edge_last, turn[j + 1], moved)
                    else:
                        coef = cy[(2, 1, 0)[j % 3]]
                        moved = turn[j]
                        if j % 3 != 0:
                            moved = jnp.where(edge_first, turn[j - 1], moved)
                    value = ws[:, cut[j]] + cx * near_x[:, cut[j]]
                    value = value + coef * moved
                    if up_z:
                        if j + 2 < tiles:
                            value = value + cz * jnp.where(low_lanes, halfway[j + 1], halfway[j + 2])
                        elif j + 1 < tiles:
                            value = value + cz * jnp.where(low_lanes, halfway[j + 1], 0.0)
                    else:
                        if j >= 2:
                            value = value + cz * jnp.where(low_lanes, halfway[j - 2], halfway[j - 1])
                        elif j >= 1:
                            value = value + cz * jnp.where(low_lanes, 0.0, halfway[j - 1])
                    if step == 0:
                        diagonal = csum + rate[:, cut[j]]
                        guess = pl.reciprocal(diagonal, approx=True)
                        inverse = guess * (2.0 - diagonal * guess)
                        recips.append(inverse)
                    else:
                        inverse = recip[:, cut[j]]
                    value = value * inverse
                    results.append(value)
                    share = base[:, cut[j]] * value
                    if step == 0:
                        acc_b[j] = acc_b[j] + share
                    acc_g[j] = acc_g[j] + share * (excess[:, cut[j]] - warm[:, cut[j]])
                target[d, own, rows, :] = jnp.concatenate(results, axis=1)
                if step == 0:
                    R[d, x, rows, :] = jnp.concatenate(recips, axis=1)
            return acc_b, acc_g

        def sweep(step, forward_y):
            def layer(i, carry):
                @pl.when(i == last)
                def _():
                    halo_wait_recv(step)

                for side in range(2):
                    x = i if side == 0 else last - i

                    def pairs(k, accs):
                        acc_b, acc_g = list(accs[0]), list(accs[1])
                        for up in range(2):
                            acc_b, acc_g = slab(
                                step, forward_y, side, 2 * k + up, up == 0, x, acc_b, acc_g
                            )
                        return (tuple(acc_b), tuple(acc_g))

                    zero = tuple(jnp.zeros((SUB, LANES), jnp.float32) for _ in range(tiles))
                    acc_b, acc_g = lax.fori_loop(0, half // 2, pairs, (zero, zero))
                    if step == 0:
                        ACCB[x] = ACCB[x] + jnp.concatenate(acc_b, axis=1)
                    ACCG[x] = ACCG[x] + jnp.concatenate(acc_g, axis=1)
                    if step:
                        out_copy(side, x).start()
                if step == 0:

                    @pl.when(i == 0)
                    def _():
                        halo_start(1)

                return carry

            lax.fori_loop(0, nx, layer, 0)

        def out_copy(side, x):
            return pltpu.make_async_copy(
                A.at[pl.ds(side * half, half), x + side],
                out.at[pl.ds(side * half, half), x],
                out_sem.at[side, x],
            )

        def both(step):
            @pl.when(ahead)
            def _():
                sweep(step, True)

            @pl.when(jnp.logical_not(ahead))
            def _():
                sweep(step, False)

        both(0)
        for x in range(nx):
            summed = jnp.sum(ACCB[x], axis=0, keepdims=True)
            XB[2, block, x : x + 1, :] = summed * (0.2 + 0.8 * denv[x : x + 1, :])
        exchange_start(2)
        exchange_middle(2)
        set_source(exchange_end(2))
        halo_wait_send(0)
        both(1)
        for x in range(nx):
            XB[3, block, x : x + 1, :] = 0.8 * jnp.sum(ACCG[x], axis=0, keepdims=True)
        exchange_start(3)
        exchange_middle(3)
        gradv[...] = exchange_end(3) * (-0.125 / ITERS)
        final = pltpu.make_async_copy(gradv, grad, grad_sem)
        final.start()
        for n in range(4):
            exchange_drain(n)
        halo_wait_send(1)
        for side in range(2):
            for x in range(nx):
                out_copy(side, x).wait()
        final.wait()

    return kernel


def solution(mesh):
    n_space, n_dir, n_band = mesh.shape["space"], mesh.shape["dir"], mesh.shape["band"]
    placed = (
        P("dir", "band", "space", None),
        P("dir", "band", "space", None),
        P("space", None),
        P("space", None),
        P(None, "band"),
        P("band"),
        P(),
        P("space", None),
    )

    def on_device(adj, pri, den, mat, rt, gs, hc, ow):
        ndir, nbands, nx, plane = adj.shape
        half = ndir // 2
        f32 = jnp.float32
        vmem = lambda *shape: pltpu.VMEM(shape, f32)
        dma = pltpu.SemaphoreType.DMA
        call = pl.pallas_call(
            make_kernel(ndir, nbands, nx, plane, n_space, n_dir, n_band),
            out_shape=(
                jax.ShapeDtypeStruct((ndir, nx, nbands, plane), f32),
                jax.ShapeDtypeStruct((nx, plane), f32),
            ),
            in_specs=[pl.BlockSpec(memory_space=pl.ANY)] * 8,
            out_specs=(pl.BlockSpec(memory_space=pl.ANY),) * 2,
            scratch_shapes=[
                vmem(ndir, nx + 1, nbands, plane),
                vmem(ndir, nx, nbands, plane),
                vmem(ndir, nx + 1, nbands, plane),
                vmem(ndir, nx, nbands, plane),
                vmem(nx, nbands, plane),
                vmem(nx, nbands, plane),
                vmem(nx, nbands, plane),
                vmem(half, 6, nbands, LANES),
                vmem(nx, nbands, plane),
                vmem(nx, nbands, plane),
                vmem(nx, SUB, plane),
                vmem(nx, SUB, plane),
                vmem(nx, SUB, plane),
                vmem(nx, plane),
                pltpu.VMEM((nx, plane), jnp.int32),
                vmem(*rt.shape),
                vmem(1, nbands),
                vmem(1, NB),
                vmem(nx, plane),
                vmem(nx, plane),
                vmem(4, n_dir, nx, plane),
                vmem(4, n_band, nx, plane),
                dma((2, 4)),
                dma((6,)),
                dma((2, 2)),
                dma((2, 2)),
                dma((4, n_dir - 1)),
                dma((4, n_dir - 1)),
                dma((4,)),
                dma((4,)),
                dma((2, nx)),
                dma,
            ],
            compiler_params=pltpu.CompilerParams(
                collective_id=0, has_side_effects=True, vmem_limit_bytes=60 * 1024 * 1024
            ),
        )
        turn = lambda v: jnp.transpose(v, (0, 2, 1, 3))
        dual, grad = call(
            turn(adj), turn(pri), den, mat, rt, gs.reshape(1, nbands), hc.reshape(1, NB), ow
        )
        return turn(dual), grad

    return jax.shard_map(
        on_device,
        mesh=mesh,
        in_specs=placed,
        out_specs=(P("dir", "band", "space", None), P("space", None)),
        check_vma=False,
    )
```

time: 199 us -> 58.1 us (0.29)
  the two profiles are of different devices: /device:TPU:32 before, /device:TPU:0 now
where the time goes in v1:
time: 58.1 us; the launch traced here: 58 us
  Pallas kernels  50.3 us (87%)
  local copies, waits for them, and re-layouts  7.08 us (12%)
  between operations  0.65 us (1%)
    pallas_call x1, Pallas kernels, on_device(): call(turn(adj), turn(pri), den, mat, rt, gs.reshape(1, nbands), hc.reshap...  50.3 us
    unnamed x4, local copies, waits for them, and re-layouts  7.08 us

profile of v1, /device:TPU:0, one launch (start us, length us, event | category | flops | bytes accessed | tf_op | source)
XLA Modules:
  0.0 58.0 jit_solution(16447454470185280995)
XLA Ops:
  0.6 50.3 %shard_map.95 = (f32[16,6,16,1152]{3,2,1,0:T(8,128)}, f32[6,1152]{1,0:T(8,128)}) custom-call(f32[16,6,16,1152]{3,2,1,0:T(8,128)} %bitcast.6, f32[16,6,16,1152]{3,2,1,0:T(8,128)} %bitcast.7, f32[6,1152]{1,0:T(8,128)} %den.1, s32[6,1152]{1,0:T(8,128)} %mat.1, f32[4,16]{1,0:T(4,128)} %rt.1, f32[1,16]{1,0:T(1,128)} %bitcast.8, f32[1,32]{1,0:T(1,128)} %bitcast.9, ...), custom_call_target="tpu_custom_call" | custom-call | tf_op jit(solution)/shard_map/pallas_call | solution.py:526
  50.9 0.0 copy-start
  50.9 6.5 %copy.12 = f32[16,16,6,1152]{3,1,2,0:T(8,128)} copy(f32[16,16,6,1152]{3,1,2,0:T(8,128)} %bitcast.5) | data formatting | bytes 14155776
  57.4 0.0 copy-done
  57.4 0.6 %copy.13 = f32[6,1152]{1,0:T(8,128)} copy(f32[6,1152]{1,0:T(8,128)S(1)} %copy-done) | data formatting | bytes 55296
Async XLA Ops:
  50.9 6.5 %copy-start = (f32[6,1152]{1,0:T(8,128)S(1)}, f32[6,1152]{1,0:T(8,128)}, u32[]{:S(2)}) copy-start(f32[6,1152]{1,0:T(8,128)} %get-tuple-element.9) | copy-start | bytes 82948

commit v2 on v1

v2 whole, which is shorter than its diff:
```python
import jax
import jax.numpy as jnp
import numpy as np
from jax import lax
from jax.experimental import pallas as pl
from jax.experimental.pallas import tpu as pltpu
from jax.sharding import PartitionSpec as P

NDIR = 64
NB = 32
NY = 192
ITERS = 2
LANES = 128
SUB = 8
MIDDLE0 = 3
MIDDLE1 = 2
MESH = pl.DeviceIdType.MESH


def direction_constants(half, blocks):
    index = np.arange(blocks * half, dtype=np.float32)
    azimuth = np.float32(np.pi) * (index + np.float32(0.5)) / np.float32(NDIR // 2)
    azimuth = azimuth - np.float32(np.pi / 2)
    pair = np.arange(blocks * half) % half
    along_z = np.float32(0.4) * (1 - 2 * (pair % 2)).astype(np.float32)
    tilt = np.sqrt(np.float32(1.0) - along_z * along_z)
    along_x = np.abs(tilt * np.cos(azimuth))
    along_y = np.abs(tilt * np.sin(azimuth))
    return (
        along_x.reshape(blocks, half),
        along_y.reshape(blocks, half),
        np.abs(along_z).reshape(blocks, half),
    )


def by_block(block, values):
    chosen = jnp.float32(values[-1])
    for index in range(len(values) - 2, -1, -1):
        chosen = jnp.where(block == index, jnp.float32(values[index]), chosen)
    return chosen


def make_kernel(ndir, nbands, nx, plane, n_space, n_dir, n_band):
    half = ndir // 2
    tiles = plane // LANES
    subs = nbands // SUB
    last = nx - 1
    const_x, const_y, const_z = direction_constants(half, n_dir)

    def kernel(
        adj, pri, den, mat, rt, gs, hc, ow,
        out, grad,
        A, PV, D, R, RATE, BASE, WS, CF, SUMA, SUMP, SUMR, SUMG, TB, SV, SH, HS, HR,
        denv, matv, rtv, gsv, hcv, owv,
        XB, ZB,
        load_sem, small_sem, h_send, h_recv, r_send, r_recv, x_send, x_recv, z_send, z_recv,
    ):
        space = lax.axis_index("space")
        block = lax.axis_index("dir")
        band = lax.axis_index("band")
        other_band = 1 - band
        has_low = space > 0
        has_high = space < n_space - 1

        barrier = pltpu.get_barrier_semaphore()
        for k in range(1, n_dir):
            peer = lax.rem(block + k, n_dir)
            pl.semaphore_signal(barrier, inc=1, device_id={"dir": peer}, device_id_type=MESH)
        pl.semaphore_signal(barrier, inc=1, device_id={"band": other_band}, device_id_type=MESH)

        @pl.when(has_low)
        def _():
            pl.semaphore_signal(barrier, inc=1, device_id={"space": space - 1}, device_id_type=MESH)

        @pl.when(has_high)
        def _():
            pl.semaphore_signal(barrier, inc=1, device_id={"space": space + 1}, device_id_type=MESH)

        smalls = [
            pltpu.make_async_copy(src, dst, small_sem.at[i])
            for i, (src, dst) in enumerate(
                ((den, denv), (mat, matv), (rt, rtv), (gs, gsv), (hc, hcv), (ow, owv))
            )
        ]
        group = 4
        loads_a = []
        loads_p = []
        for g in range(ndir // group):
            first = g * group
            shift = 0 if first < half else 1
            loads_a.append(
                pltpu.make_async_copy(
                    adj.at[pl.ds(first, group)],
                    A.at[pl.ds(first, group), pl.ds(shift, nx)],
                    load_sem.at[0, g],
                )
            )
            loads_p.append(
                pltpu.make_async_copy(
                    pri.at[pl.ds(first, group)], PV.at[pl.ds(first, group)], load_sem.at[1, g]
                )
            )
        for copy in smalls:
            copy.start()
        for copy in loads_a:
            copy.start()
        for copy in loads_p:
            copy.start()

        with jax.named_scope("barrier"):
            at_end = jnp.logical_or(space == 0, space == n_space - 1)

            @pl.when(at_end)
            def _():
                pl.semaphore_wait(barrier, n_dir + 1)

            @pl.when(jnp.logical_not(at_end))
            def _():
                pl.semaphore_wait(barrier, n_dir + 2)

        def beside(src, dst, down, send_sem, recv_sem):
            return pltpu.make_async_remote_copy(
                src_ref=src,
                dst_ref=dst,
                send_sem=send_sem,
                recv_sem=recv_sem,
                device_id={"space": space - 1 if down else space + 1},
                device_id_type=MESH,
            )

        def halo(step, down):
            way = 0 if down else 1
            rows = pl.ds(0 if down else half, half)
            buffer = D if step else A
            if step:
                src = D.at[rows, 0 if down else nx]
            else:
                src = adj.at[rows, 0 if down else last]
            dst = buffer.at[rows, nx if down else 0]
            return beside(src, dst, down, h_send.at[step, way], h_recv.at[step, way])

        def rows_copy(step, down):
            way = 0 if down else 1
            if step == 0:
                src, dst = HS.at[way], HR.at[way]
            else:
                src, dst = SV.at[0 if down else last], SH.at[way]
            return beside(src, dst, down, r_send.at[step, way], r_recv.at[step, way])

        def both_ways(make, act, receive=False):
            @pl.when(has_high if receive else has_low)
            def _():
                act(make(True))

            @pl.when(has_low if receive else has_high)
            def _():
                act(make(False))

        def start(make):
            both_ways(make, lambda copy: copy.start())

        def arrive(make):
            both_ways(make, lambda copy: copy.wait_recv(), receive=True)

        def drain(make):
            both_ways(make, lambda copy: copy.wait_send())

        with jax.named_scope("halo0"):
            start(lambda down: halo(0, down))

        @pl.when(jnp.logical_not(has_high))
        def _():
            def clear(d, carry):
                for buffer in (A, D, R):
                    buffer[d, nx] = jnp.zeros((nbands, plane), jnp.float32)
                return carry

            lax.fori_loop(0, half, clear, 0)

        @pl.when(jnp.logical_not(has_low))
        def _():
            def clear(d, carry):
                for buffer in (A, D, R):
                    buffer[half + d, 0] = jnp.zeros((nbands, plane), jnp.float32)
                return carry

            lax.fori_loop(0, half, clear, 0)

        with jax.named_scope("smallwait"):
            for copy in smalls:
                copy.wait()
        with jax.named_scope("tables"):
            for way, x in ((0, 0), (1, last)):
                HS[way, 0] = denv[x : x + 1, :]
                HS[way, 1] = matv[x : x + 1, :].astype(jnp.float32)
            start(lambda down: rows_copy(0, down))
            row_index = lax.broadcasted_iota(jnp.int32, (nbands, nbands), 0)
            lane_index = lax.broadcasted_iota(jnp.int32, (nbands, nbands), 1)

            def column(row):
                spread = jnp.where(row_index == lane_index, row, 0.0)
                return jnp.broadcast_to(jnp.sum(spread, axis=1, keepdims=True), (nbands, LANES))

            rates = [column(rtv[m : m + 1, :]) for m in range(rt.shape[0])]
            speed = column(gsv[...])
            heat = hcv[...]
            total_heat = jnp.sum(heat, axis=1, keepdims=True)
            wide_row = lax.broadcasted_iota(jnp.int32, (nbands, NB), 0) + band * nbands
            wide_lane = lax.broadcasted_iota(jnp.int32, (nbands, NB), 1)
            local_heat = jnp.sum(jnp.where(wide_row == wide_lane, heat, 0.0), axis=1, keepdims=True)
            weight = jnp.broadcast_to(local_heat / (NDIR * total_heat), (nbands, LANES))
            wide_weight = jnp.concatenate([weight] * tiles, axis=1)
            lane = lax.broadcasted_iota(jnp.int32, (nbands, LANES), 1)
            ahead = block >= n_dir // 2
            middle = jnp.where(ahead, 63, 64)
            edge = jnp.where(ahead, LANES - 1, 0)
            for pair in range(half):
                sx = speed * by_block(block, const_x[:, pair])
                sy = speed * by_block(block, const_y[:, pair])
                sz = speed * jnp.float32(const_z[0, pair])
                CF[pair, 0] = sx
                CF[pair, 1] = sy
                CF[pair, 2] = jnp.where(lane == middle, 0.0, sy)
                CF[pair, 3] = jnp.where(lane == edge, 0.0, sy)
                CF[pair, 4] = sz
                CF[pair, 5] = sx + sy + sz

            def base_of(kind_row, j):
                kind = jnp.broadcast_to(kind_row, (nbands, LANES))
                base = rates[-1]
                for m in range(rt.shape[0] - 2, -1, -1):
                    base = jnp.where(kind == m, rates[m], base)
                return base

            cuts = [slice(j * LANES, (j + 1) * LANES) for j in range(tiles)]
            for x in range(nx):
                for j in range(tiles):
                    base = base_of(matv[x : x + 1, cuts[j]], j)
                    BASE[x, :, cuts[j]] = base
                    RATE[x, :, cuts[j]] = base * (0.2 + 0.8 * denv[x : x + 1, cuts[j]])

        def sum_group(source, target, g, shift):
            def body(x, carry):
                total = source[g * group, x + shift]
                for d in range(1, group):
                    total = total + source[g * group + d, x + shift]
                if g:
                    total = total + target[x]
                target[x] = total
                return carry

            lax.fori_loop(0, nx, body, 0)

        def x_copy(n, k):
            ref = XB.at[n, block] if n < 2 else XB.at[n, block, 0]
            return pltpu.make_async_remote_copy(
                src_ref=ref,
                dst_ref=ref,
                send_sem=x_send.at[n, k - 1],
                recv_sem=x_recv.at[n, k - 1],
                device_id={"dir": lax.rem(block + k, n_dir)},
                device_id_type=MESH,
            )

        def z_copy(n):
            ref = ZB.at[n, band] if n < 2 else ZB.at[n, band, 0]
            return pltpu.make_async_remote_copy(
                src_ref=ref,
                dst_ref=ref,
                send_sem=z_send.at[n],
                recv_sem=z_recv.at[n],
                device_id={"band": other_band},
                device_id_type=MESH,
            )

        def exchange_start(n):
            for k in range(1, n_dir):
                x_copy(n, k).start()

        def exchange_middle(n):
            for k in range(1, n_dir):
                x_copy(n, k).wait_recv()
            for part in range(2 if n < 2 else 1):
                total = XB[n, 0, part]
                for k in range(1, n_dir):
                    total = total + XB[n, k, part]
                ZB[n, band, part] = total
            z_copy(n).start()

        def exchange_end(n):
            z_copy(n).wait_recv()
            return [ZB[n, 0, part] + ZB[n, 1, part] for part in range(2 if n < 2 else 1)]

        def exchange_drain(n):
            for k in range(1, n_dir):
                x_copy(n, k).wait_send()
            z_copy(n).wait_send()

        def fold(n, part, x, value):
            XB[n, block, part, x : x + 1, :] = jnp.sum(value, axis=0, keepdims=True)

        with jax.named_scope("sum_a"):
            for g in range(ndir // group):
                loads_a[g].wait()
                sum_group(A, SUMA, g, 0 if g * group < half else 1)
            for x in range(nx):
                fold(0, 0, x, RATE[x] * SUMA[x])
        with jax.named_scope("sum_p"):
            for g in range(ndir // group):
                loads_p[g].wait()
                sum_group(PV, SUMP, g, 0)
            for x in range(nx):
                fold(0, 1, x, wide_weight * SUMP[x])
            exchange_start(0)

        for x in range(nx):
            for buffer in (SUMA, SUMR, SUMP, SUMG):
                buffer[x] = jnp.zeros((nbands, plane), jnp.float32)

        lane8 = lax.broadcasted_iota(jnp.int32, (SUB, LANES), 1)
        low_lanes = lane8 < LANES // 2
        edge_first = lane8 == 0
        edge_last = lane8 == LANES - 1

        def reciprocal(diagonal):
            guess = pl.reciprocal(diagonal, approx=True)
            return guess * (2.0 - diagonal * guess)

        def stream(forward_y, up_z, pair, rows, field, near_x):
            cx = CF[pair, 0, rows, :]
            cy = [CF[pair, 1 + i, rows, :] for i in range(3)]
            cz = CF[pair, 4, rows, :]
            turn = [pltpu.roll(v, LANES - 1 if forward_y else 1, 1) for v in field]
            halfway = [pltpu.roll(v, LANES // 2, 1) for v in field]
            values = []
            for j in range(tiles):
                moved = turn[j]
                if forward_y:
                    coef = cy[(0, 1, 2)[j % 3]]
                    if j % 3 != 2:
                        moved = jnp.where(edge_last, turn[j + 1], moved)
                else:
                    coef = cy[(2, 1, 0)[j % 3]]
                    if j % 3 != 0:
                        moved = jnp.where(edge_first, turn[j - 1], moved)
                value = cx * near_x[j] + coef * moved
                if up_z:
                    if j + 2 < tiles:
                        value = value + cz * jnp.where(low_lanes, halfway[j + 1], halfway[j + 2])
                    elif j + 1 < tiles:
                        value = value + cz * jnp.where(low_lanes, halfway[j + 1], 0.0)
                else:
                    if j >= 2:
                        value = value + cz * jnp.where(low_lanes, halfway[j - 2], halfway[j - 1])
                    elif j >= 1:
                        value = value + cz * jnp.where(low_lanes, 0.0, halfway[j - 1])
                values.append(value)
            return values

        def split(ref_rows):
            return [ref_rows[:, c] for c in cuts]

        def join(parts):
            return jnp.concatenate(parts, axis=1)

        def slab_a(forward_y, side, x):
            for s in range(subs):
                rows = pl.ds(s * SUB, SUB)
                rate = split(RATE[x, rows, :])
                total_a, total_r = None, None
                for pair in range(half):
                    d = pair + side * half
                    own, other = x + side, x + 1 - side
                    csum = CF[pair, 5, rows, :]
                    near = stream(
                        forward_y, pair % 2 == 0, pair, rows, split(A[d, own, rows, :]), split(A[d, other, rows, :])
                    )
                    inverse = [reciprocal(csum + rate[j]) for j in range(tiles)]
                    value = join([near[j] * inverse[j] for j in range(tiles)])
                    inverse = join(inverse)
                    D[d, own, rows, :] = value
                    R[d, own, rows, :] = inverse
                    total_a = value if pair == 0 else total_a + value
                    total_r = inverse if pair == 0 else total_r + inverse
                SUMA[x, rows, :] = SUMA[x, rows, :] + total_a
                SUMR[x, rows, :] = SUMR[x, rows, :] + total_r

        def slab_b(forward_y, side, x):
            warm = split(TB[x])
            for s in range(subs):
                rows = pl.ds(s * SUB, SUB)
                source = split(WS[x + 2 - 2 * side, rows, :])
                own_source = split(WS[x + 1, rows, :])
                total_g, total_e = None, None
                for pair in range(half):
                    d = pair + side * half
                    own, other = x + side, x + 1 - side
                    beside_a = split(D[d, other, rows, :])
                    beside_r = split(R[d, other, rows, :])
                    near_x = [beside_a[j] + source[j] * beside_r[j] for j in range(tiles)]
                    own_a = split(D[d, own, rows, :])
                    inverse = split(R[d, own, rows, :])
                    field = [own_a[j] + own_source[j] * inverse[j] for j in range(tiles)]
                    near = stream(forward_y, pair % 2 == 0, pair, rows, field, near_x)
                    value = [near[j] * inverse[j] for j in range(tiles)]
                    out[d, x, rows, :] = join(value)
                    excess = split(PV[d, x, rows, :])
                    excess = [excess[j] - warm[j] for j in range(tiles)]
                    part_g = [(field[j] + value[j]) * excess[j] for j in range(tiles)]
                    part_e = [inverse[j] * excess[j] for j in range(tiles)]
                    total_g = part_g if pair == 0 else [total_g[j] + part_g[j] for j in range(tiles)]
                    total_e = part_e if pair == 0 else [total_e[j] + part_e[j] for j in range(tiles)]
                SUMG[x, rows, :] = SUMG[x, rows, :] + join(total_g)
                SUMP[x, rows, :] = SUMP[x, rows, :] + join(total_e)

        def sweep(step, forward_y, hooks):
            def layer(i, carry):
                for at, hook in hooks["before"].items():
                    pl.when(i == at)(hook)
                for side in range(2):
                    x = i if side == 0 else last - i
                    (slab_b if step else slab_a)(forward_y, side, x)
                for at, hook in hooks["after"].items():
                    pl.when(i == at)(hook)
                return carry

            lax.fori_loop(0, nx, layer, 0)

        def both(step, hooks):
            @pl.when(ahead)
            def _():
                sweep(step, True, hooks)

            @pl.when(jnp.logical_not(ahead))
            def _():
                sweep(step, False, hooks)

        def set_source(x, slot, row):
            WS[slot] = wide_weight * row

        def wait_halo0():
            with jax.named_scope("waithalo0"):
                arrive(lambda down: halo(0, down))

        late_down = space == n_space // 2
        late_up = space == n_space // 2 - 1

        def send_halo1():
            @pl.when(jnp.logical_and(has_low, jnp.logical_not(late_down)))
            def _():
                halo(1, True).start()

            @pl.when(jnp.logical_and(has_high, jnp.logical_not(late_up)))
            def _():
                halo(1, False).start()

        def send_halo1_late():
            @pl.when(late_down)
            def _():
                halo(1, True).start()

            @pl.when(late_up)
            def _():
                halo(1, False).start()

        def middle0():
            with jax.named_scope("middle0"):
                exchange_middle(0)

        with jax.named_scope("sweepA"):
            both(0, {"before": {last: wait_halo0}, "after": {0: send_halo1, MIDDLE0: middle0}})
        with jax.named_scope("fold1"):
            for x in range(nx):
                fold(1, 0, x, BASE[x] * SUMA[x])
                fold(1, 1, x, BASE[x] * wide_weight * SUMR[x])
            exchange_start(1)

        with jax.named_scope("halodiag"):
            arrive(lambda down: rows_copy(0, down))

            def halo_diagonal(way):
                own = nx if way == 0 else 0
                for j in range(tiles):
                    base = base_of(HR[way, 1, :, cuts[j]], j)
                    rate = base * (0.2 + 0.8 * HR[way, 0, :, cuts[j]])
                    for pair in range(half):
                        R[pair + way * half, own, :, cuts[j]] = reciprocal(CF[pair, 5] + rate)

            @pl.when(has_high)
            def _():
                halo_diagonal(0)

            @pl.when(has_low)
            def _():
                halo_diagonal(1)

        with jax.named_scope("end0"):
            coupling, temperature = exchange_end(0)
        send_halo1_late()
        with jax.named_scope("source0"):
            cell_source = NDIR * NB * owv[...]
            first_source = coupling + cell_source
            for x in range(nx):
                SV[x] = first_source[x : x + 1]
            start(lambda down: rows_copy(1, down))
            for x in range(nx):
                WS[x + 1] = wide_weight * first_source[x : x + 1]
                TB[x] = jnp.broadcast_to(temperature[x : x + 1], (SUB, plane))

        def wait_halo1():
            with jax.named_scope("waithalo1"):
                arrive(lambda down: halo(1, down))
                arrive(lambda down: rows_copy(1, down))

                @pl.when(has_high)
                def _():
                    WS[nx + 1] = wide_weight * SH[0]

                @pl.when(jnp.logical_not(has_high))
                def _():
                    WS[nx + 1] = jnp.zeros((nbands, plane), jnp.float32)

                @pl.when(has_low)
                def _():
                    WS[0] = wide_weight * SH[1]

                @pl.when(jnp.logical_not(has_low))
                def _():
                    WS[0] = jnp.zeros((nbands, plane), jnp.float32)

        def middle1():
            with jax.named_scope("middle1"):
                exchange_middle(1)

        with jax.named_scope("sweepB"):
            both(1, {"before": {last: wait_halo1}, "after": {MIDDLE1: middle1}})
        with jax.named_scope("end1"):
            first, second = exchange_end(1)
        with jax.named_scope("fold2"):
            scale = 0.2 + 0.8 * denv[...]
            second_source = scale * (first + first_source * second) + cell_source
            for x in range(nx):
                source = wide_weight * second_source[x : x + 1]
                WS[x + 1] = source
                fold(2, 0, x, 0.8 * BASE[x] * (SUMG[x] + source * SUMP[x]))
            exchange_start(2)

        with jax.named_scope("final"):

            def finish(x, carry):
                source = WS[x + 1]
                for d in range(ndir):
                    out[d, x] = out[d, x] + source * R[d, x + (0 if d < half else 1)]
                return carry

            lax.fori_loop(0, nx, finish, 0)
        with jax.named_scope("exch2"):
            exchange_middle(2)
            grad[...] = exchange_end(2)[0] * (-0.125 / ITERS)
        with jax.named_scope("drain"):
            for n in range(3):
                exchange_drain(n)
            for step in range(2):
                drain(lambda down: halo(step, down))
                drain(lambda down: rows_copy(step, down))

    return kernel


def solution(mesh):
    n_space, n_dir, n_band = mesh.shape["space"], mesh.shape["dir"], mesh.shape["band"]
    placed = (
        P("dir", "band", "space", None),
        P("dir", "band", "space", None),
        P("space", None),
        P("space", None),
        P(None, "band"),
        P("band"),
        P(),
        P("space", None),
    )

    def on_device(adj, pri, den, mat, rt, gs, hc, ow):
        ndir, nbands, nx, plane = adj.shape
        half = ndir // 2
        f32 = jnp.float32
        vmem = lambda *shape: pltpu.VMEM(shape, f32)
        dma = pltpu.SemaphoreType.DMA
        call = pl.pallas_call(
            make_kernel(ndir, nbands, nx, plane, n_space, n_dir, n_band),
            out_shape=(
                jax.ShapeDtypeStruct((ndir, nx, nbands, plane), f32),
                jax.ShapeDtypeStruct((nx, plane), f32),
            ),
            in_specs=[pl.BlockSpec(memory_space=pltpu.HBM)] * 8,
            out_specs=(pl.BlockSpec(memory_space=pltpu.VMEM),) * 2,
            scratch_shapes=[
                vmem(ndir, nx + 1, nbands, plane),
                vmem(ndir, nx, nbands, plane),
                vmem(ndir, nx + 1, nbands, plane),
                vmem(ndir, nx + 1, nbands, plane),
                vmem(nx, nbands, plane),
                vmem(nx, nbands, plane),
                vmem(nx + 2, nbands, plane),
                vmem(half, 6, nbands, LANES),
                vmem(nx, nbands, plane),
                vmem(nx, nbands, plane),
                vmem(nx, nbands, plane),
                vmem(nx, nbands, plane),
                vmem(nx, SUB, plane),
                vmem(nx, 1, plane),
                vmem(2, 1, plane),
                vmem(2, 2, 1, plane),
                vmem(2, 2, 1, plane),
                vmem(nx, plane),
                pltpu.VMEM((nx, plane), jnp.int32),
                vmem(*rt.shape),
                vmem(1, nbands),
                vmem(1, NB),
                vmem(nx, plane),
                vmem(3, n_dir, 2, nx, plane),
                vmem(3, n_band, 2, nx, plane),
                dma((2, 4)),
                dma((6,)),
                dma((2, 2)),
                dma((2, 2)),
                dma((2, 2)),
                dma((2, 2)),
                dma((3, n_dir - 1)),
                dma((3, n_dir - 1)),
                dma((3,)),
                dma((3,)),
            ],
            compiler_params=pltpu.CompilerParams(
                collective_id=0, has_side_effects=True, vmem_limit_bytes=40 * 1024 * 1024
            ),
        )
        turn = lambda v: jnp.transpose(v, (0, 2, 1, 3))
        operands = (
            turn(adj), turn(pri), den, mat, rt, gs.reshape(1, nbands), hc.reshape(1, NB), ow
        )
        dual, grad = call(*[pltpu.with_memory_space_constraint(v, pltpu.HBM) for v in operands])
        return turn(dual), grad

    return jax.shard_map(
        on_device,
        mesh=mesh,
        in_specs=placed,
        out_specs=(P("dir", "band", "space", None), P("space", None)),
        check_vma=False,
    )
```

time: 58.1 us -> 43 us (0.74)
  Pallas kernels: 50.3 us -> 38.7 us
  local copies, waits for them, and re-layouts: 7.08 us -> 3.58 us
    pallas_call x1, Pallas kernels: 50.3 us -> 38.7 us  [on_device(): call(*[pltpu.with_memory_space_constraint(v, pltpu.HBM) for v in operands])]
    unnamed x4 -> x2, local copies, waits for them, and re-layouts: 7.08 us -> 3.58 us
where the time goes in v2:
time: 43 us; the launch traced here: 42.9 us
  Pallas kernels  38.7 us (90%)
  local copies, waits for them, and re-layouts  3.58 us (8%)
  between operations  0.64 us (1%)
    pallas_call x1, Pallas kernels, on_device(): call(*[pltpu.with_memory_space_constraint(v, pltpu.HBM) for v in operands])  38.7 us
    unnamed x2, local copies, waits for them, and re-layouts  3.58 us

profile of v2, /device:TPU:0, one launch (start us, length us, event | category | flops | bytes accessed | tf_op | source)
XLA Modules:
  0.0 42.9 jit_solution(18013985452819056436)
XLA Ops:
  0.6 38.7 %shard_map.95 = (f32[16,6,16,1152]{3,2,1,0:T(8,128)S(1)}, f32[6,1152]{1,0:T(8,128)S(1)}) custom-call(f32[16,6,16,1152]{3,2,1,0:T(8,128)} %bitcast.6, f32[16,6,16,1152]{3,2,1,0:T(8,128)} %bitcast.7, f32[6,1152]{1,0:T(8,128)} %den.1, s32[6,1152]{1,0:T(8,128)} %mat.1, f32[4,16]{1,0:T(4,128)} %rt.1, f32[1,16]{1,0:T(1,128)} %bitcast.8, f32[1,32]{1,0:T(1,128)} %bitcast.9, ...), custom_call_target="tpu_custom_call" | custom-call | tf_op jit(solution)/shard_map/pallas_call | solution.py:642
  39.3 3.0 %copy.12 = f32[16,16,6,1152]{3,1,2,0:T(8,128)} copy(f32[16,16,6,1152]{3,1,2,0:T(8,128)S(1)} %bitcast.5) | data formatting | bytes 14155776
  42.3 0.6 %copy.13 = f32[6,1152]{1,0:T(8,128)} copy(f32[6,1152]{1,0:T(8,128)S(1)} %get-tuple-element.9) | data formatting | bytes 55296

commit v3 on v2

--- a/solution.py
+++ b/solution.py
@@ -12,7 +12,11 @@
 ITERS = 2
 LANES = 128
 SUB = 8
+SECOND = 2
+THIRD = 3
+LAST = 4
 MIDDLE0 = 3
+MIDDLET = 0
 MIDDLE1 = 2
 MESH = pl.DeviceIdType.MESH
 
@@ -51,7 +55,7 @@
         adj, pri, den, mat, rt, gs, hc, ow,
         out, grad,
         A, PV, D, R, RATE, BASE, WS, CF, SUMA, SUMP, SUMR, SUMG, TB, SV, SH, HS, HR,
-        denv, matv, rtv, gsv, hcv, owv,
+        denv, matv, rtv, gsv, hcv, owv, TL,
         XB, ZB,
         load_sem, small_sem, h_send, h_recv, r_send, r_recv, x_send, x_recv, z_send, z_recv,
     ):
@@ -66,7 +70,15 @@
         for k in range(1, n_dir):
             peer = lax.rem(block + k, n_dir)
             pl.semaphore_signal(barrier, inc=1, device_id={"dir": peer}, device_id_type=MESH)
+        before, after = lax.rem(block + n_dir - 1, n_dir), lax.rem(block + 1, n_dir)
         pl.semaphore_signal(barrier, inc=1, device_id={"band": other_band}, device_id_type=MESH)
+        shared = jnp.logical_or(space < 2, space >= n_space - 2)
+
+        @pl.when(shared)
+        def _():
+            pl.semaphore_signal(
+                barrier, inc=1, device_id={"dir": after, "band": other_band}, device_id_type=MESH
+            )
 
         @pl.when(has_low)
         def _():
@@ -102,21 +114,6 @@
             )
         for copy in smalls:
             copy.start()
-        for copy in loads_a:
-            copy.start()
-        for copy in loads_p:
-            copy.start()
-
-        with jax.named_scope("barrier"):
-            at_end = jnp.logical_or(space == 0, space == n_space - 1)
-
-            @pl.when(at_end)
-            def _():
-                pl.semaphore_wait(barrier, n_dir + 1)
-
-            @pl.when(jnp.logical_not(at_end))
-            def _():
-                pl.semaphore_wait(barrier, n_dir + 2)
 
         def beside(src, dst, down, send_sem, recv_sem):
             return pltpu.make_async_remote_copy(
@@ -165,14 +162,12 @@
         def drain(make):
             both_ways(make, lambda copy: copy.wait_send())
 
-        with jax.named_scope("halo0"):
-            start(lambda down: halo(0, down))
-
         @pl.when(jnp.logical_not(has_high))
         def _():
             def clear(d, carry):
-                for buffer in (A, D, R):
+                for buffer in (A, D):
                     buffer[d, nx] = jnp.zeros((nbands, plane), jnp.float32)
+                R[d, nx + 1] = jnp.zeros((nbands, plane), jnp.float32)
                 return carry
 
             lax.fori_loop(0, half, clear, 0)
@@ -180,8 +175,9 @@
         @pl.when(jnp.logical_not(has_low))
         def _():
             def clear(d, carry):
-                for buffer in (A, D, R):
+                for buffer in (A, D):
                     buffer[half + d, 0] = jnp.zeros((nbands, plane), jnp.float32)
+                R[d, 0] = jnp.zeros((nbands, plane), jnp.float32)
                 return carry
 
             lax.fori_loop(0, half, clear, 0)
@@ -189,11 +185,14 @@
         with jax.named_scope("smallwait"):
             for copy in smalls:
                 copy.wait()
+            for copy in loads_a:
+                copy.start()
+            for copy in loads_p:
+                copy.start()
         with jax.named_scope("tables"):
             for way, x in ((0, 0), (1, last)):
                 HS[way, 0] = denv[x : x + 1, :]
                 HS[way, 1] = matv[x : x + 1, :].astype(jnp.float32)
-            start(lambda down: rows_copy(0, down))
             row_index = lax.broadcasted_iota(jnp.int32, (nbands, nbands), 0)
             lane_index = lax.broadcasted_iota(jnp.int32, (nbands, nbands), 1)
 
@@ -210,6 +209,7 @@
             local_heat = jnp.sum(jnp.where(wide_row == wide_lane, heat, 0.0), axis=1, keepdims=True)
             weight = jnp.broadcast_to(local_heat / (NDIR * total_heat), (nbands, LANES))
             wide_weight = jnp.concatenate([weight] * tiles, axis=1)
+            mean_scale = 1.0 / (ndir * jnp.sum(weight, axis=0, keepdims=True))
             lane = lax.broadcasted_iota(jnp.int32, (nbands, LANES), 1)
             ahead = block >= n_dir // 2
             middle = jnp.where(ahead, 63, 64)
@@ -239,6 +239,43 @@
                     BASE[x, :, cuts[j]] = base
                     RATE[x, :, cuts[j]] = base * (0.2 + 0.8 * denv[x : x + 1, cuts[j]])
 
+        def reciprocal(diagonal):
+            guess = pl.reciprocal(diagonal, approx=True)
+            return guess * (2.0 - diagonal * guess)
+
+        with jax.named_scope("diagonal"):
+
+            def diagonals(x, carry):
+                for s in range(subs):
+                    rows = pl.ds(s * SUB, SUB)
+                    rate = RATE[x, rows, :]
+                    total = None
+                    for pair in range(half):
+                        csum = jnp.concatenate([CF[pair, 5, rows, :]] * tiles, axis=1)
+                        inverse = reciprocal(csum + rate)
+                        R[pair, x + 1, rows, :] = inverse
+                        total = inverse if pair == 0 else total + inverse
+                    SUMR[x, rows, :] = total + total
+                return carry
+
+            lax.fori_loop(0, nx, diagonals, 0)
+
+        with jax.named_scope("barrier"):
+            most = jnp.logical_or(space == 1, space == n_space - 2)
+
+            @pl.when(most)
+            def _():
+                pl.semaphore_wait(barrier, n_dir + 3)
+
+            @pl.when(jnp.logical_not(most))
+            def _():
+                pl.semaphore_wait(barrier, n_dir + 2)
+
+        with jax.named_scope("halo0"):
+            start(lambda down: halo(0, down))
+
+        start(lambda down: rows_copy(0, down))
+
         def sum_group(source, target, g, shift):
             def body(x, carry):
                 total = source[g * group, x + shift]
@@ -252,7 +289,7 @@
             lax.fori_loop(0, nx, body, 0)
 
         def x_copy(n, k):
-            ref = XB.at[n, block] if n < 2 else XB.at[n, block, 0]
+            ref = XB.at[n, block]
             return pltpu.make_async_remote_copy(
                 src_ref=ref,
                 dst_ref=ref,
@@ -262,69 +299,84 @@
                 device_id_type=MESH,
             )
 
-        def z_copy(n):
-            ref = ZB.at[n, band] if n < 2 else ZB.at[n, band, 0]
+        def z_copy(n, aside=False):
+            ref = ZB.at[n, band]
             return pltpu.make_async_remote_copy(
                 src_ref=ref,
                 dst_ref=ref,
                 send_sem=z_send.at[n],
                 recv_sem=z_recv.at[n],
-                device_id={"band": other_band},
+                device_id={"dir": before if aside else block, "band": other_band},
                 device_id_type=MESH,
             )
 
-        def exchange_start(n):
+        def x_start(n):
             for k in range(1, n_dir):
                 x_copy(n, k).start()
 
-        def exchange_middle(n):
+        def x_end(n):
             for k in range(1, n_dir):
                 x_copy(n, k).wait_recv()
-            for part in range(2 if n < 2 else 1):
-                total = XB[n, 0, part]
-                for k in range(1, n_dir):
-                    total = total + XB[n, k, part]
-                ZB[n, band, part] = total
-            z_copy(n).start()
+            total = XB[n, 0]
+            for k in range(1, n_dir):
+                total = total + XB[n, k]
+            return total
+
+        def x_then_z(n):
+            ZB[n, band] = x_end(n)
+            if n == LAST:
+                z_copy(n).start()
+            else:
+
+                @pl.when(shared)
+                def _():
+                    z_copy(n, True).start()
+
+                @pl.when(jnp.logical_not(shared))
+                def _():
+                    z_copy(n).start()
 
         def exchange_end(n):
             z_copy(n).wait_recv()
-            return [ZB[n, 0, part] + ZB[n, 1, part] for part in range(2 if n < 2 else 1)]
+            return ZB[n, 0] + ZB[n, 1]
 
         def exchange_drain(n):
             for k in range(1, n_dir):
                 x_copy(n, k).wait_send()
             z_copy(n).wait_send()
 
-        def fold(n, part, x, value):
-            XB[n, block, part, x : x + 1, :] = jnp.sum(value, axis=0, keepdims=True)
+        def folded(value):
+            return jnp.sum(value, axis=0, keepdims=True)
 
         with jax.named_scope("sum_a"):
             for g in range(ndir // group):
                 loads_a[g].wait()
                 sum_group(A, SUMA, g, 0 if g * group < half else 1)
             for x in range(nx):
-                fold(0, 0, x, RATE[x] * SUMA[x])
+                XB[0, block, x : x + 1, :] = folded(RATE[x] * SUMA[x])
+            x_start(0)
+            for x in range(nx):
+                XB[THIRD, block, x : x + 1, :] = folded(BASE[x] * wide_weight * SUMR[x])
+            x_start(THIRD)
         with jax.named_scope("sum_p"):
             for g in range(ndir // group):
                 loads_p[g].wait()
                 sum_group(PV, SUMP, g, 0)
             for x in range(nx):
-                fold(0, 1, x, wide_weight * SUMP[x])
-            exchange_start(0)
+                share = folded(wide_weight * SUMP[x])
+                XB[1, block, x : x + 1, :] = share
+                TL[x : x + 1, :] = share * mean_scale[:, :1]
+                TB[x] = jnp.broadcast_to(TL[x : x + 1, :], (SUB, plane))
+            x_start(1)
 
         for x in range(nx):
-            for buffer in (SUMA, SUMR, SUMP, SUMG):
+            for buffer in (SUMA, SUMP, SUMG):
                 buffer[x] = jnp.zeros((nbands, plane), jnp.float32)
 
         lane8 = lax.broadcasted_iota(jnp.int32, (SUB, LANES), 1)
         low_lanes = lane8 < LANES // 2
         edge_first = lane8 == 0
         edge_last = lane8 == LANES - 1
-
-        def reciprocal(diagonal):
-            guess = pl.reciprocal(diagonal, approx=True)
-            return guess * (2.0 - diagonal * guess)
 
         def stream(forward_y, up_z, pair, rows, field, near_x):
             cx = CF[pair, 0, rows, :]
@@ -366,24 +418,17 @@
         def slab_a(forward_y, side, x):
             for s in range(subs):
                 rows = pl.ds(s * SUB, SUB)
-                rate = split(RATE[x, rows, :])
-                total_a, total_r = None, None
+                total = None
                 for pair in range(half):
                     d = pair + side * half
                     own, other = x + side, x + 1 - side
-                    csum = CF[pair, 5, rows, :]
                     near = stream(
                         forward_y, pair % 2 == 0, pair, rows, split(A[d, own, rows, :]), split(A[d, other, rows, :])
                     )
-                    inverse = [reciprocal(csum + rate[j]) for j in range(tiles)]
-                    value = join([near[j] * inverse[j] for j in range(tiles)])
-                    inverse = join(inverse)
+                    value = join(near) * R[pair, x + 1, rows, :]
                     D[d, own, rows, :] = value
-                    R[d, own, rows, :] = inverse
-                    total_a = value if pair == 0 else total_a + value
-                    total_r = inverse if pair == 0 else total_r + inverse
-                SUMA[x, rows, :] = SUMA[x, rows, :] + total_a
-                SUMR[x, rows, :] = SUMR[x, rows, :] + total_r
+                    total = value if pair == 0 else total + value
+                SUMA[x, rows, :] = SUMA[x, rows, :] + total
 
         def slab_b(forward_y, side, x):
             warm = split(TB[x])
@@ -391,27 +436,30 @@
                 rows = pl.ds(s * SUB, SUB)
                 source = split(WS[x + 2 - 2 * side, rows, :])
                 own_source = split(WS[x + 1, rows, :])
-                total_g, total_e = None, None
+                total_g, total_e, total_h = None, None, None
                 for pair in range(half):
                     d = pair + side * half
                     own, other = x + side, x + 1 - side
                     beside_a = split(D[d, other, rows, :])
-                    beside_r = split(R[d, other, rows, :])
+                    beside_r = split(R[pair, x + 2 - 2 * side, rows, :])
                     near_x = [beside_a[j] + source[j] * beside_r[j] for j in range(tiles)]
                     own_a = split(D[d, own, rows, :])
-                    inverse = split(R[d, own, rows, :])
+                    inverse = split(R[pair, x + 1, rows, :])
                     field = [own_a[j] + own_source[j] * inverse[j] for j in range(tiles)]
                     near = stream(forward_y, pair % 2 == 0, pair, rows, field, near_x)
                     value = [near[j] * inverse[j] for j in range(tiles)]
                     out[d, x, rows, :] = join(value)
                     excess = split(PV[d, x, rows, :])
                     excess = [excess[j] - warm[j] for j in range(tiles)]
-                    part_g = [(field[j] + value[j]) * excess[j] for j in range(tiles)]
+                    both_duals = [field[j] + value[j] for j in range(tiles)]
+                    part_g = [both_duals[j] * excess[j] for j in range(tiles)]
                     part_e = [inverse[j] * excess[j] for j in range(tiles)]
                     total_g = part_g if pair == 0 else [total_g[j] + part_g[j] for j in range(tiles)]
                     total_e = part_e if pair == 0 else [total_e[j] + part_e[j] for j in range(tiles)]
+                    total_h = both_duals if pair == 0 else [total_h[j] + both_duals[j] for j in range(tiles)]
                 SUMG[x, rows, :] = SUMG[x, rows, :] + join(total_g)
                 SUMP[x, rows, :] = SUMP[x, rows, :] + join(total_e)
+                SUMA[x, rows, :] = SUMA[x, rows, :] + join(total_h)
 
         def sweep(step, forward_y, hooks):
             def layer(i, carry):
@@ -442,49 +490,36 @@
             with jax.named_scope("waithalo0"):
                 arrive(lambda down: halo(0, down))
 
-        late_down = space == n_space // 2
-        late_up = space == n_space // 2 - 1
-
         def send_halo1():
-            @pl.when(jnp.logical_and(has_low, jnp.logical_not(late_down)))
-            def _():
-                halo(1, True).start()
-
-            @pl.when(jnp.logical_and(has_high, jnp.logical_not(late_up)))
-            def _():
-                halo(1, False).start()
-
-        def send_halo1_late():
-            @pl.when(late_down)
-            def _():
-                halo(1, True).start()
-
-            @pl.when(late_up)
-            def _():
-                halo(1, False).start()
+            start(lambda down: halo(1, down))
 
         def middle0():
             with jax.named_scope("middle0"):
-                exchange_middle(0)
+                x_then_z(0)
+
+        def middle_t():
+            with jax.named_scope("middleT"):
+                x_then_z(THIRD)
+                x_then_z(1)
 
         with jax.named_scope("sweepA"):
             both(0, {"before": {last: wait_halo0}, "after": {0: send_halo1, MIDDLE0: middle0}})
         with jax.named_scope("fold1"):
             for x in range(nx):
-                fold(1, 0, x, BASE[x] * SUMA[x])
-                fold(1, 1, x, BASE[x] * wide_weight * SUMR[x])
-            exchange_start(1)
+                XB[SECOND, block, x : x + 1, :] = folded(BASE[x] * SUMA[x])
+                SUMA[x] = jnp.zeros((nbands, plane), jnp.float32)
+            x_start(SECOND)
 
         with jax.named_scope("halodiag"):
             arrive(lambda down: rows_copy(0, down))
 
             def halo_diagonal(way):
-                own = nx if way == 0 else 0
+                own = nx + 1 if way == 0 else 0
                 for j in range(tiles):
                     base = base_of(HR[way, 1, :, cuts[j]], j)
                     rate = base * (0.2 + 0.8 * HR[way, 0, :, cuts[j]])
                     for pair in range(half):
-                        R[pair + way * half, own, :, cuts[j]] = reciprocal(CF[pair, 5] + rate)
+                        R[pair, own, :, cuts[j]] = reciprocal(CF[pair, 5] + rate)
 
             @pl.when(has_high)
             def _():
@@ -495,17 +530,17 @@
                 halo_diagonal(1)
 
         with jax.named_scope("end0"):
-            coupling, temperature = exchange_end(0)
-        send_halo1_late()
+            coupling = exchange_end(0)
         with jax.named_scope("source0"):
             cell_source = NDIR * NB * owv[...]
             first_source = coupling + cell_source
             for x in range(nx):
                 SV[x] = first_source[x : x + 1]
             start(lambda down: rows_copy(1, down))
-            for x in range(nx):
-                WS[x + 1] = wide_weight * first_source[x : x + 1]
-                TB[x] = jnp.broadcast_to(temperature[x : x + 1], (SUB, plane))
+        with jax.named_scope("source1"):
+            for x in range(nx):
+                source = wide_weight * first_source[x : x + 1]
+                WS[x + 1] = source
 
         def wait_halo1():
             with jax.named_scope("waithalo1"):
@@ -530,35 +565,44 @@
 
         def middle1():
             with jax.named_scope("middle1"):
-                exchange_middle(1)
+                x_then_z(SECOND)
 
         with jax.named_scope("sweepB"):
-            both(1, {"before": {last: wait_halo1}, "after": {MIDDLE1: middle1}})
+            both(1, {"before": {last: wait_halo1}, "after": {MIDDLET: middle_t, MIDDLE1: middle1}})
         with jax.named_scope("end1"):
-            first, second = exchange_end(1)
+            first_source = SV[:, 0]
+            total = exchange_end(SECOND) + first_source * exchange_end(THIRD)
+            temperature = exchange_end(1)
+            shift = temperature - TL[...]
         with jax.named_scope("fold2"):
             scale = 0.2 + 0.8 * denv[...]
-            second_source = scale * (first + first_source * second) + cell_source
+            second_source = scale * total + NDIR * NB * owv[...]
             for x in range(nx):
                 source = wide_weight * second_source[x : x + 1]
                 WS[x + 1] = source
-                fold(2, 0, x, 0.8 * BASE[x] * (SUMG[x] + source * SUMP[x]))
-            exchange_start(2)
+                XB[LAST, block, x : x + 1, :] = folded(
+                    0.8
+                    * BASE[x]
+                    * (SUMG[x] + source * SUMP[x] - shift[x : x + 1] * (SUMA[x] + source * SUMR[x]))
+                )
+            x_start(LAST)
 
         with jax.named_scope("final"):
 
             def finish(x, carry):
                 source = WS[x + 1]
                 for d in range(ndir):
-                    out[d, x] = out[d, x] + source * R[d, x + (0 if d < half else 1)]
+                    out[d, x] = out[d, x] + source * R[d % half, x + 1]
                 return carry
 
             lax.fori_loop(0, nx, finish, 0)
         with jax.named_scope("exch2"):
-            exchange_middle(2)
-            grad[...] = exchange_end(2)[0] * (-0.125 / ITERS)
+            with jax.named_scope("last_x"):
+                x_then_z(LAST)
+            with jax.named_scope("last_z"):
+                grad[...] = exchange_end(LAST) * (-0.125 / ITERS)
         with jax.named_scope("drain"):
-            for n in range(3):
+            for n in range(5):
                 exchange_drain(n)
             for step in range(2):
                 drain(lambda down: halo(step, down))
@@ -598,7 +642,7 @@
                 vmem(ndir, nx + 1, nbands, plane),
                 vmem(ndir, nx, nbands, plane),
                 vmem(ndir, nx + 1, nbands, plane),
-                vmem(ndir, nx + 1, nbands, plane),
+                vmem(half, nx + 2, nbands, plane),
                 vmem(nx, nbands, plane),
                 vmem(nx, nbands, plane),
                 vmem(nx + 2, nbands, plane),
@@ -618,18 +662,19 @@
                 vmem(1, nbands),
                 vmem(1, NB),
                 vmem(nx, plane),
-                vmem(3, n_dir, 2, nx, plane),
-                vmem(3, n_band, 2, nx, plane),
+                vmem(nx, plane),
+                vmem(5, n_dir, nx, plane),
+                vmem(5, n_band, nx, plane),
                 dma((2, 4)),
                 dma((6,)),
                 dma((2, 2)),
                 dma((2, 2)),
                 dma((2, 2)),
                 dma((2, 2)),
-                dma((3, n_dir - 1)),
-                dma((3, n_dir - 1)),
-                dma((3,)),
-                dma((3,)),
+                dma((5, n_dir - 1)),
+                dma((5, n_dir - 1)),
+                dma((5,)),
+                dma((5,)),
             ],
             compiler_params=pltpu.CompilerParams(
                 collective_id=0, has_side_effects=True, vmem_limit_bytes=40 * 1024 * 1024

time: 43 us -> 39.3 us (0.914)
  Pallas kernels: 38.7 us -> 34.9 us
    pallas_call x1, Pallas kernels: 38.7 us -> 34.9 us  [on_device(): call(*[pltpu.with_memory_space_constraint(v, pltpu.HBM) for v in operands])]
where the time goes in v3:
time: 39.3 us; the launch traced here: 39.1 us
  Pallas kernels  34.9 us (89%)
  local copies, waits for them, and re-layouts  3.58 us (9%)
  between operations  0.64 us (2%)
    pallas_call x1, Pallas kernels, on_device(): call(*[pltpu.with_memory_space_constraint(v, pltpu.HBM) for v in operands])  34.9 us
    unnamed x2, local copies, waits for them, and re-layouts  3.58 us

profile of v3, /device:TPU:0, one launch (start us, length us, event | category | flops | bytes accessed | tf_op | source)
XLA Modules:
  0.0 39.1 jit_solution(6773075537954800329)
XLA Ops:
  0.6 34.9 %shard_map.95 = (f32[16,6,16,1152]{3,2,1,0:T(8,128)S(1)}, f32[6,1152]{1,0:T(8,128)S(1)}) custom-call(f32[16,6,16,1152]{3,2,1,0:T(8,128)} %bitcast.6, f32[16,6,16,1152]{3,2,1,0:T(8,128)} %bitcast.7, f32[6,1152]{1,0:T(8,128)} %den.1, s32[6,1152]{1,0:T(8,128)} %mat.1, f32[4,16]{1,0:T(4,128)} %rt.1, f32[1,16]{1,0:T(1,128)} %bitcast.8, f32[1,32]{1,0:T(1,128)} %bitcast.9, ...), custom_call_target="tpu_custom_call" | custom-call | tf_op jit(solution)/shard_map/pallas_call | solution.py:687
  35.5 3.0 %copy.12 = f32[16,16,6,1152]{3,1,2,0:T(8,128)} copy(f32[16,16,6,1152]{3,1,2,0:T(8,128)S(1)} %bitcast.5) | data formatting | bytes 14155776
  38.5 0.6 %copy.13 = f32[6,1152]{1,0:T(8,128)} copy(f32[6,1152]{1,0:T(8,128)S(1)} %get-tuple-element.9) | data formatting | bytes 55296

commit v4 on v3

--- a/solution.py
+++ b/solution.py
@@ -14,9 +14,9 @@
 SUB = 8
 SECOND = 2
 THIRD = 3
-LAST = 4
+EARLY = 4
+LATE = 5
 MIDDLE0 = 3
-MIDDLET = 0
 MIDDLE1 = 2
 MESH = pl.DeviceIdType.MESH
 
@@ -55,14 +55,15 @@
         adj, pri, den, mat, rt, gs, hc, ow,
         out, grad,
         A, PV, D, R, RATE, BASE, WS, CF, SUMA, SUMP, SUMR, SUMG, TB, SV, SH, HS, HR,
-        denv, matv, rtv, gsv, hcv, owv, TL,
-        XB, ZB,
+        denv, matv, rtv, gsv, hcv, owv, TL, SH_T,
+        XB, ZB, XE, XL, ZE, ZL,
         load_sem, small_sem, h_send, h_recv, r_send, r_recv, x_send, x_recv, z_send, z_recv,
     ):
         space = lax.axis_index("space")
         block = lax.axis_index("dir")
         band = lax.axis_index("band")
         other_band = 1 - band
+        odd = lax.rem(space, 2)
         has_low = space > 0
         has_high = space < n_space - 1
 
@@ -154,7 +155,17 @@
                 act(make(False))
 
         def start(make):
-            both_ways(make, lambda copy: copy.start())
+            @pl.when(jnp.logical_and(has_high, odd == 1))
+            def _():
+                make(False).start()
+
+            @pl.when(has_low)
+            def _():
+                make(True).start()
+
+            @pl.when(jnp.logical_and(has_high, odd == 0))
+            def _():
+                make(False).start()
 
         def arrive(make):
             both_ways(make, lambda copy: copy.wait_recv(), receive=True)
@@ -289,7 +300,7 @@
             lax.fori_loop(0, nx, body, 0)
 
         def x_copy(n, k):
-            ref = XB.at[n, block]
+            ref = XE.at[block] if n == EARLY else XL.at[block] if n == LATE else XB.at[n, block]
             return pltpu.make_async_remote_copy(
                 src_ref=ref,
                 dst_ref=ref,
@@ -300,7 +311,7 @@
             )
 
         def z_copy(n, aside=False):
-            ref = ZB.at[n, band]
+            ref = ZE.at[band] if n == EARLY else ZL.at[band] if n == LATE else ZB.at[n, band]
             return pltpu.make_async_remote_copy(
                 src_ref=ref,
                 dst_ref=ref,
@@ -317,16 +328,24 @@
         def x_end(n):
             for k in range(1, n_dir):
                 x_copy(n, k).wait_recv()
-            total = XB[n, 0]
-            for k in range(1, n_dir):
-                total = total + XB[n, k]
+            terms = [
+                XE[k] if n == EARLY else XL[k] if n == LATE else XB[n, k] for k in range(n_dir)
+            ]
+            total = terms[0]
+            for term in terms[1:]:
+                total = total + term
             return total
 
         def x_then_z(n):
-            ZB[n, band] = x_end(n)
-            if n == LAST:
+            total = x_end(n)
+            if n == EARLY:
+                ZE[band] = total
+                z_copy(n).start()
+            elif n == LATE:
+                ZL[band] = total
                 z_copy(n).start()
             else:
+                ZB[n, band] = total
 
                 @pl.when(shared)
                 def _():
@@ -338,6 +357,10 @@
 
         def exchange_end(n):
             z_copy(n).wait_recv()
+            if n == EARLY:
+                return ZE[0] + ZE[1]
+            if n == LATE:
+                return ZL[0] + ZL[1]
             return ZB[n, 0] + ZB[n, 1]
 
         def exchange_drain(n):
@@ -468,7 +491,7 @@
                 for side in range(2):
                     x = i if side == 0 else last - i
                     (slab_b if step else slab_a)(forward_y, side, x)
-                for at, hook in hooks["after"].items():
+                for at, hook in hooks["after"]:
                     pl.when(i == at)(hook)
                 return carry
 
@@ -499,11 +522,11 @@
 
         def middle_t():
             with jax.named_scope("middleT"):
+                x_then_z(1)
                 x_then_z(THIRD)
-                x_then_z(1)
 
         with jax.named_scope("sweepA"):
-            both(0, {"before": {last: wait_halo0}, "after": {0: send_halo1, MIDDLE0: middle0}})
+            both(0, {"before": {last: wait_halo0}, "after": ((0, send_halo1), (MIDDLE0, middle0))})
         with jax.named_scope("fold1"):
             for x in range(nx):
                 XB[SECOND, block, x : x + 1, :] = folded(BASE[x] * SUMA[x])
@@ -529,6 +552,7 @@
             def _():
                 halo_diagonal(1)
 
+        middle_t()
         with jax.named_scope("end0"):
             coupling = exchange_end(0)
         with jax.named_scope("source0"):
@@ -567,26 +591,36 @@
             with jax.named_scope("middle1"):
                 x_then_z(SECOND)
 
+        def gradient_sums(x):
+            base = 0.8 * BASE[x]
+            shift = SH_T[x : x + 1, :]
+            slope = folded(base * (SUMG[x] - shift * SUMA[x]))
+            return slope, folded(base * wide_weight * (SUMP[x] - shift * SUMR[x]))
+
+        def send_early():
+            with jax.named_scope("early"):
+                SH_T[...] = exchange_end(1) - TL[...]
+                for row in range(nx - 2):
+                    slope, share = gradient_sums(row + 1)
+                    XE[block, row : row + 1, :] = slope
+                    XE[block, nx - 2 + row : nx - 1 + row, :] = share
+                x_start(EARLY)
+
         with jax.named_scope("sweepB"):
-            both(1, {"before": {last: wait_halo1}, "after": {MIDDLET: middle_t, MIDDLE1: middle1}})
+            both(1, {"before": {last: wait_halo1}, "after": ((MIDDLE1 + 1 * odd, middle1), (last - 1, send_early))})
+        with jax.named_scope("late"):
+            for row, x in ((0, 0), (1, last)):
+                slope, share = gradient_sums(x)
+                XL[block, row : row + 1, :] = slope
+                XL[block, 2 + row : 3 + row, :] = share
+            x_start(LATE)
         with jax.named_scope("end1"):
             first_source = SV[:, 0]
             total = exchange_end(SECOND) + first_source * exchange_end(THIRD)
-            temperature = exchange_end(1)
-            shift = temperature - TL[...]
-        with jax.named_scope("fold2"):
             scale = 0.2 + 0.8 * denv[...]
             second_source = scale * total + NDIR * NB * owv[...]
             for x in range(nx):
-                source = wide_weight * second_source[x : x + 1]
-                WS[x + 1] = source
-                XB[LAST, block, x : x + 1, :] = folded(
-                    0.8
-                    * BASE[x]
-                    * (SUMG[x] + source * SUMP[x] - shift[x : x + 1] * (SUMA[x] + source * SUMR[x]))
-                )
-            x_start(LAST)
-
+                WS[x + 1] = wide_weight * second_source[x : x + 1]
         with jax.named_scope("final"):
 
             def finish(x, carry):
@@ -596,19 +630,34 @@
                 return carry
 
             lax.fori_loop(0, nx, finish, 0)
-        with jax.named_scope("exch2"):
-            with jax.named_scope("last_x"):
-                x_then_z(LAST)
-            with jax.named_scope("last_z"):
-                grad[...] = exchange_end(LAST) * (-0.125 / ITERS)
+        with jax.named_scope("early_x"):
+            x_then_z(EARLY)
+        with jax.named_scope("late_x"):
+            x_then_z(LATE)
+        with jax.named_scope("last_z"):
+            inner, outer = exchange_end(EARLY), exchange_end(LATE)
+            slope = jnp.concatenate([outer[0:1], inner[: nx - 2], outer[1:2]], axis=0)
+            share = jnp.concatenate([outer[2:3], inner[nx - 2 :], outer[3:4]], axis=0)
+            grad[...] = (slope + second_source * share) * (-0.125 / ITERS)
         with jax.named_scope("drain"):
-            for n in range(5):
+            for n in range(6):
                 exchange_drain(n)
             for step in range(2):
                 drain(lambda down: halo(step, down))
                 drain(lambda down: rows_copy(step, down))
 
     return kernel
+
+
+def write_out(dual, grad, dual_out, grad_out, sem):
+    count = dual.shape[0]
+    copies = [pltpu.make_async_copy(grad, grad_out, sem.at[count])]
+    for d in range(count):
+        copies.append(pltpu.make_async_copy(dual.at[d], dual_out.at[d], sem.at[d]))
+    for copy in copies:
+        copy.start()
+    for copy in copies:
+        copy.wait()
 
 
 def solution(mesh):
@@ -663,18 +712,23 @@
                 vmem(1, NB),
                 vmem(nx, plane),
                 vmem(nx, plane),
-                vmem(5, n_dir, nx, plane),
-                vmem(5, n_band, nx, plane),
+                vmem(nx, plane),
+                vmem(4, n_dir, nx, plane),
+                vmem(4, n_band, nx, plane),
+                vmem(n_dir, 2 * (nx - 2), plane),
+                vmem(n_dir, 4, plane),
+                vmem(n_band, 2 * (nx - 2), plane),
+                vmem(n_band, 4, plane),
                 dma((2, 4)),
                 dma((6,)),
                 dma((2, 2)),
                 dma((2, 2)),
                 dma((2, 2)),
                 dma((2, 2)),
-                dma((5, n_dir - 1)),
-                dma((5, n_dir - 1)),
-                dma((5,)),
-                dma((5,)),
+                dma((6, n_dir - 1)),
+                dma((6, n_dir - 1)),
+                dma((6,)),
+                dma((6,)),
             ],
             compiler_params=pltpu.CompilerParams(
                 collective_id=0, has_side_effects=True, vmem_limit_bytes=40 * 1024 * 1024
@@ -685,6 +739,17 @@
             turn(adj), turn(pri), den, mat, rt, gs.reshape(1, nbands), hc.reshape(1, NB), ow
         )
         dual, grad = call(*[pltpu.with_memory_space_constraint(v, pltpu.HBM) for v in operands])
+        dual, grad = pl.pallas_call(
+            write_out,
+            out_shape=(
+                jax.ShapeDtypeStruct(dual.shape, f32),
+                jax.ShapeDtypeStruct(grad.shape, f32),
+            ),
+            in_specs=[pl.BlockSpec(memory_space=pltpu.VMEM)] * 2,
+            out_specs=(pl.BlockSpec(memory_space=pltpu.HBM),) * 2,
+            scratch_shapes=[dma((ndir + 1,))],
+            compiler_params=pltpu.CompilerParams(vmem_limit_bytes=1024 * 1024),
+        )(dual, grad)
         return turn(dual), grad
 
     return jax.shard_map(

time: 39.3 us -> 37.3 us (0.949)
  the two profiles are of different devices: /device:TPU:0 before, /device:TPU:32 now
where the time goes in v4:
time: 37.3 us; the launch traced here: 37.1 us
  Pallas kernels  36.4 us (98%)
  between operations  0.64 us (2%)
    pallas_call x1, Pallas kernels, on_device(): call(*[pltpu.with_memory_space_constraint(v, pltpu.HBM) for v in operands])  33.4 us
    pallas_call x1, Pallas kernels, on_device(): pl.pallas_call(write_out, out_shape=(jax.ShapeDtypeStruct(dual.shape, f32...  3.04 us

profile of v4, /device:TPU:32, one launch (start us, length us, event | category | flops | bytes accessed | tf_op | source)
XLA Modules:
  0.0 37.1 jit_solution(3617307481737222202)
XLA Ops:
  0.6 33.4 %shard_map.95 = (f32[16,6,16,1152]{3,2,1,0:T(8,128)S(1)}, f32[6,1152]{1,0:T(8,128)S(1)}) custom-call(f32[16,6,16,1152]{3,2,1,0:T(8,128)} %bitcast.5, f32[16,6,16,1152]{3,2,1,0:T(8,128)} %bitcast.6, f32[6,1152]{1,0:T(8,128)} %den.1, s32[6,1152]{1,0:T(8,128)} %mat.1, f32[4,16]{1,0:T(4,128)} %rt.1, f32[1,16]{1,0:T(1,128)} %bitcast.7, f32[1,32]{1,0:T(1,128)} %bitcast.8, ...), custom_call_target="tpu_custom_call" | custom-call | tf_op jit(solution)/shard_map/pallas_call | solution.py:741
  34.0 3.0 %shard_map.96 = (f32[16,6,16,1152]{3,2,1,0:T(8,128)}, f32[6,1152]{1,0:T(8,128)}) custom-call(f32[16,6,16,1152]{3,2,1,0:T(8,128)S(1)} %get-tuple-element.6.dual, f32[6,1152]{1,0:T(8,128)S(1)} %get-tuple-element.7.grad), custom_call_target="tpu_custom_call" | custom-call | tf_op jit(solution)/shard_map/pallas_call | solution.py:742

commit v5 on v4

--- a/solution.py
+++ b/solution.py
@@ -154,18 +154,27 @@
             def _():
                 act(make(False))
 
+        def start_far(make):
+            @pl.when(jnp.logical_and(has_high, odd == 1))
+            def _():
+                make(False).start()
+
+            @pl.when(jnp.logical_and(has_low, odd == 0))
+            def _():
+                make(True).start()
+
+        def start_near(make):
+            @pl.when(odd == 1)
+            def _():
+                make(True).start()
+
+            @pl.when(odd == 0)
+            def _():
+                make(False).start()
+
         def start(make):
-            @pl.when(jnp.logical_and(has_high, odd == 1))
-            def _():
-                make(False).start()
-
-            @pl.when(has_low)
-            def _():
-                make(True).start()
-
-            @pl.when(jnp.logical_and(has_high, odd == 0))
-            def _():
-                make(False).start()
+            start_far(make)
+            start_near(make)
 
         def arrive(make):
             both_ways(make, lambda copy: copy.wait_recv(), receive=True)
@@ -283,7 +292,7 @@
                 pl.semaphore_wait(barrier, n_dir + 2)
 
         with jax.named_scope("halo0"):
-            start(lambda down: halo(0, down))
+            start_far(lambda down: halo(0, down))
 
         start(lambda down: rows_copy(0, down))
 
@@ -380,7 +389,6 @@
             x_start(0)
             for x in range(nx):
                 XB[THIRD, block, x : x + 1, :] = folded(BASE[x] * wide_weight * SUMR[x])
-            x_start(THIRD)
         with jax.named_scope("sum_p"):
             for g in range(ndir // group):
                 loads_p[g].wait()
@@ -486,9 +494,8 @@
 
         def sweep(step, forward_y, hooks):
             def layer(i, carry):
-                for at, hook in hooks["before"].items():
-                    pl.when(i == at)(hook)
                 for side in range(2):
+                    pl.when(i == last)(hooks["halo"][side])
                     x = i if side == 0 else last - i
                     (slab_b if step else slab_a)(forward_y, side, x)
                 for at, hook in hooks["after"]:
@@ -509,24 +516,31 @@
         def set_source(x, slot, row):
             WS[slot] = wide_weight * row
 
-        def wait_halo0():
-            with jax.named_scope("waithalo0"):
-                arrive(lambda down: halo(0, down))
+        def wait_halo0(side):
+            def hook():
+                @pl.when(has_low if side else has_high)
+                def _():
+                    halo(0, side == 0).wait_recv()
+
+            return hook
 
         def send_halo1():
-            start(lambda down: halo(1, down))
+            start_far(lambda down: halo(1, down))
+
+        def send_near0():
+            start_near(lambda down: halo(0, down))
 
         def middle0():
             with jax.named_scope("middle0"):
                 x_then_z(0)
+                x_start(THIRD)
 
         def middle_t():
             with jax.named_scope("middleT"):
                 x_then_z(1)
-                x_then_z(THIRD)
 
         with jax.named_scope("sweepA"):
-            both(0, {"before": {last: wait_halo0}, "after": ((0, send_halo1), (MIDDLE0, middle0))})
+            both(0, {"halo": [wait_halo0(0), wait_halo0(1)], "after": ((1, send_near0), (0, send_halo1), (MIDDLE0, middle0))})
         with jax.named_scope("fold1"):
             for x in range(nx):
                 XB[SECOND, block, x : x + 1, :] = folded(BASE[x] * SUMA[x])
@@ -555,6 +569,7 @@
         middle_t()
         with jax.named_scope("end0"):
             coupling = exchange_end(0)
+        start_near(lambda down: halo(1, down))
         with jax.named_scope("source0"):
             cell_source = NDIR * NB * owv[...]
             first_source = coupling + cell_source
@@ -566,30 +581,27 @@
                 source = wide_weight * first_source[x : x + 1]
                 WS[x + 1] = source
 
-        def wait_halo1():
-            with jax.named_scope("waithalo1"):
-                arrive(lambda down: halo(1, down))
-                arrive(lambda down: rows_copy(1, down))
-
-                @pl.when(has_high)
-                def _():
-                    WS[nx + 1] = wide_weight * SH[0]
-
-                @pl.when(jnp.logical_not(has_high))
-                def _():
-                    WS[nx + 1] = jnp.zeros((nbands, plane), jnp.float32)
-
-                @pl.when(has_low)
-                def _():
-                    WS[0] = wide_weight * SH[1]
-
-                @pl.when(jnp.logical_not(has_low))
-                def _():
-                    WS[0] = jnp.zeros((nbands, plane), jnp.float32)
+        def wait_halo1(side):
+            layer, row = (0, 1) if side else (nx + 1, 0)
+
+            def hook():
+                with jax.named_scope("waithalo1"):
+                    @pl.when(has_low if side else has_high)
+                    def _():
+                        halo(1, side == 0).wait_recv()
+                        rows_copy(1, side == 0).wait_recv()
+                        WS[layer] = wide_weight * SH[row]
+
+                    @pl.when(jnp.logical_not(has_low if side else has_high))
+                    def _():
+                        WS[layer] = jnp.zeros((nbands, plane), jnp.float32)
+
+            return hook
 
         def middle1():
             with jax.named_scope("middle1"):
                 x_then_z(SECOND)
+                x_then_z(THIRD)
 
         def gradient_sums(x):
             base = 0.8 * BASE[x]
@@ -607,13 +619,17 @@
                 x_start(EARLY)
 
         with jax.named_scope("sweepB"):
-            both(1, {"before": {last: wait_halo1}, "after": ((MIDDLE1 + 1 * odd, middle1), (last - 1, send_early))})
+            both(1, {"halo": [wait_halo1(0), wait_halo1(1)], "after": ((last - 1, middle1), (last - 1, send_early))})
         with jax.named_scope("late"):
             for row, x in ((0, 0), (1, last)):
                 slope, share = gradient_sums(x)
                 XL[block, row : row + 1, :] = slope
                 XL[block, 2 + row : 3 + row, :] = share
             x_start(LATE)
+        with jax.named_scope("early_x"):
+            x_then_z(EARLY)
+        with jax.named_scope("late_x"):
+            x_then_z(LATE)
         with jax.named_scope("end1"):
             first_source = SV[:, 0]
             total = exchange_end(SECOND) + first_source * exchange_end(THIRD)
@@ -630,10 +646,6 @@
                 return carry
 
             lax.fori_loop(0, nx, finish, 0)
-        with jax.named_scope("early_x"):
-            x_then_z(EARLY)
-        with jax.named_scope("late_x"):
-            x_then_z(LATE)
         with jax.named_scope("last_z"):
             inner, outer = exchange_end(EARLY), exchange_end(LATE)
             slope = jnp.concatenate([outer[0:1], inner[: nx - 2], outer[1:2]], axis=0)

time: 37.3 us -> 35.4 us (0.949)
  the two profiles are of different devices: /device:TPU:32 before, /device:TPU:0 now
where the time goes in v5:
time: 35.4 us; the launch traced here: 35 us
  Pallas kernels  34.4 us (97%)
  between operations  0.64 us (2%)
    pallas_call x1, Pallas kernels, on_device(): call(*[pltpu.with_memory_space_constraint(v, pltpu.HBM) for v in operands])  31.4 us
    pallas_call x1, Pallas kernels, on_device(): pl.pallas_call(write_out, out_shape=(jax.ShapeDtypeStruct(dual.shape, f32...  3.04 us

profile of v5, /device:TPU:0, one launch (start us, length us, event | category | flops | bytes accessed | tf_op | source)
XLA Modules:
  0.0 35.0 jit_solution(8123688854957841881)
XLA Ops:
  0.6 31.4 %shard_map.95 = (f32[16,6,16,1152]{3,2,1,0:T(8,128)S(1)}, f32[6,1152]{1,0:T(8,128)S(1)}) custom-call(f32[16,6,16,1152]{3,2,1,0:T(8,128)} %bitcast.5, f32[16,6,16,1152]{3,2,1,0:T(8,128)} %bitcast.6, f32[6,1152]{1,0:T(8,128)} %den.1, s32[6,1152]{1,0:T(8,128)} %mat.1, f32[4,16]{1,0:T(4,128)} %rt.1, f32[1,16]{1,0:T(1,128)} %bitcast.7, f32[1,32]{1,0:T(1,128)} %bitcast.8, ...), custom_call_target="tpu_custom_call" | custom-call | tf_op jit(solution)/shard_map/pallas_call | solution.py:753
  32.0 3.0 %shard_map.96 = (f32[16,6,16,1152]{3,2,1,0:T(8,128)}, f32[6,1152]{1,0:T(8,128)}) custom-call(f32[16,6,16,1152]{3,2,1,0:T(8,128)S(1)} %get-tuple-element.6.dual, f32[6,1152]{1,0:T(8,128)S(1)} %get-tuple-element.7.grad), custom_call_target="tpu_custom_call" | custom-call | tf_op jit(solution)/shard_map/pallas_call | solution.py:754

commit v6 on v5

--- a/solution.py
+++ b/solution.py
@@ -331,7 +331,7 @@
             )
 
         def x_start(n):
-            for k in range(1, n_dir):
+            for k in sorted(range(1, n_dir), key=lambda k: -min(k, n_dir - k)):
                 x_copy(n, k).start()
 
         def x_end(n):
@@ -352,6 +352,9 @@
                 z_copy(n).start()
             elif n == LATE:
                 ZL[band] = total
+                z_copy(n).start()
+            elif n >= SECOND:
+                ZB[n, band] = total
                 z_copy(n).start()
             else:
                 ZB[n, band] = total

time: 35.4 us -> 35 us (0.989)
  no operation moved by 1% of the time
where the time goes in v6:
time: 35 us; the launch traced here: 34.8 us
  Pallas kernels  34.2 us (98%)
  between operations  0.64 us (2%)
    pallas_call x1, Pallas kernels, on_device(): call(*[pltpu.with_memory_space_constraint(v, pltpu.HBM) for v in operands])  31.1 us
    pallas_call x1, Pallas kernels, on_device(): pl.pallas_call(write_out, out_shape=(jax.ShapeDtypeStruct(dual.shape, f32...  3.04 us

profile of v6, /device:TPU:0, one launch (start us, length us, event | category | flops | bytes accessed | tf_op | source)
XLA Modules:
  0.0 34.8 jit_solution(12907154998237795073)
XLA Ops:
  0.6 31.1 %shard_map.95 = (f32[16,6,16,1152]{3,2,1,0:T(8,128)S(1)}, f32[6,1152]{1,0:T(8,128)S(1)}) custom-call(f32[16,6,16,1152]{3,2,1,0:T(8,128)} %bitcast.5, f32[16,6,16,1152]{3,2,1,0:T(8,128)} %bitcast.6, f32[6,1152]{1,0:T(8,128)} %den.1, s32[6,1152]{1,0:T(8,128)} %mat.1, f32[4,16]{1,0:T(4,128)} %rt.1, f32[1,16]{1,0:T(1,128)} %bitcast.7, f32[1,32]{1,0:T(1,128)} %bitcast.8, ...), custom_call_target="tpu_custom_call" | custom-call | tf_op jit(solution)/shard_map/pallas_call | solution.py:756
  31.8 3.0 %shard_map.96 = (f32[16,6,16,1152]{3,2,1,0:T(8,128)}, f32[6,1152]{1,0:T(8,128)}) custom-call(f32[16,6,16,1152]{3,2,1,0:T(8,128)S(1)} %get-tuple-element.6.dual, f32[6,1152]{1,0:T(8,128)S(1)} %get-tuple-element.7.grad), custom_call_target="tpu_custom_call" | custom-call | tf_op jit(solution)/shard_map/pallas_call | solution.py:757
